TPU v7x, 512 devices: a whole 4x4x16 slice. The times are simulated.
512 devices in a mesh: slab: 256 (over z, y, x), col: 2 (over core).
Axes of the slice: x: 4, y: 4, z: 16, core: 2. Of those that a mesh axis runs over, the one named last changes fastest.
Arguments:
- populations: float32 [19, 512, 32, 128], P(None, 'slab', 'col'), may hold values from 0.75 to 1.5
- wall_flags: int32 [512, 32, 128], P('slab', 'col'), may hold values 0 or 1
Outputs:
- image: float32 [4, 128, 512], P(None, 'col', 'slab')
- final_populations: float32 [19, 512, 32, 128], P(None, 'slab', 'col')
Inputs may be any that keep to these rules, and one draw needn't show every extreme that they name: `wall_flags`: 1 marks a wall node, 0 a fluid node.
All inputs are finite; a program needn't handle non-finite values. No bound on the sum of `wall_flags` on one device may be relied on, other than what follows from the above.
Results may differ from a plain program's by a relative error of at most 0.00024.
Values sent between devices are 32-bit elements; how exact they have to be, the bound alone decides.
No kernel may reach another device: no remote copies, remote signals or barrier semaphores. Data moves between devices by JAX's collectives and lax.ppermute only.
A program may use at most 64 MiB of HBM per device.

v0:
```python
import jax
import jax.numpy as jnp
from jax import lax
from jax.sharding import PartitionSpec as P

STEPS = 2


lattice_dirs = (
    (0, 0, 0),
    (0, 0, 1),
    (1, 0, 1),
    (-1, 0, 1),
    (0, 1, 1),
    (0, -1, 1),
    (0, 0, -1),
    (1, 0, -1),
    (-1, 0, -1),
    (0, 1, -1),
    (0, -1, -1),
    (1, 0, 0),
    (-1, 0, 0),
    (0, 1, 0),
    (0, -1, 0),
    (1, 1, 0),
    (-1, -1, 0),
    (1, -1, 0),
    (-1, 1, 0),
)
opposite_dir = tuple(
    (lattice_dirs.index(tuple((-element for element in direction))) for direction in lattice_dirs)
)
lattice_weights = tuple(
    (
        (
            1.0 / 3.0
            if sum((abs(element) for element in direction)) == 0
            else 1.0 / 18.0 if sum((abs(element) for element in direction)) == 1 else 1.0 / 36.0
        )
        for direction in lattice_dirs
    )
)
upward_dirs = tuple(
    (dir_index for dir_index, direction in enumerate(lattice_dirs) if direction[1] == 1)
)
downward_dirs = tuple(
    (dir_index for dir_index, direction in enumerate(lattice_dirs) if direction[1] == -1)
)
speed_gain = 10000.0
optical = 2.0


def with_halo(cells, sides, width):
    for axis, dim in sides:
        count = lax.axis_size(axis)
        head = lax.slice_in_dim(cells, 0, width, axis=dim)
        tail = lax.slice_in_dim(cells, cells.shape[dim] - width, cells.shape[dim], axis=dim)
        cells = jnp.concatenate(
            [
                lax.ppermute(tail, axis, [(i, (i + 1) % count) for i in range(count)]),
                cells,
                lax.ppermute(head, axis, [((i + 1) % count, i) for i in range(count)]),
            ],
            axis=dim,
        )
    return cells


def swapped(value, axis, distance):
    mask = 2**distance
    pairs = [(source, source ^ mask) for source in range(lax.axis_size(axis))]
    return lax.ppermute(value, axis, pairs)


def moments(lattice_state):
    vel_table = jnp.asarray(lattice_dirs, dtype=jnp.float32)
    density = jnp.sum(lattice_state, axis=0)
    momentum = jnp.einsum(
        "iv,izyx->vzyx", vel_table, lattice_state, precision=lax.Precision.HIGHEST
    )
    velocity = momentum / density[None]
    speed_sq = jnp.sum(velocity * velocity, axis=0)
    return (density, velocity, speed_sq)


def relax(lattice_state, wall_flags):
    density, velocity, speed_sq = moments(lattice_state)
    vel_table = jnp.asarray(lattice_dirs, dtype=jnp.float32)
    weights = jnp.asarray(lattice_weights, dtype=jnp.float32)
    project = jnp.einsum("iv,vzyx->izyx", vel_table, velocity, precision=lax.Precision.HIGHEST)
    balance = (
        weights[:, None, None, None]
        * density[None]
        * (1.0 + 3.0 * project + 4.5 * project * project - 1.5 * speed_sq[None])
    )
    bounced = jnp.stack([lattice_state[dir_index] for dir_index in opposite_dir])
    return jnp.where(wall_flags[None] == 1, bounced, balance)


def stream_local(relaxed):
    depth_count = relaxed.shape[1]
    row_count = relaxed.shape[2]
    extended = with_halo(relaxed, (("slab", 1),), 1)
    along_z = jnp.concatenate(
        [
            extended[0:1, 1 : depth_count + 1],
            extended[1:6, 0:depth_count],
            extended[6:11, 2 : depth_count + 2],
            extended[11:, 1 : depth_count + 1],
        ],
        axis=0,
    )
    upward = jnp.stack([along_z[dir_index] for dir_index in upward_dirs])
    downward = jnp.stack([along_z[dir_index] for dir_index in downward_dirs])
    moving = jnp.concatenate([upward, downward], axis=0)
    widened = with_halo(moving, (("col", 2),), 1)
    plus_y = widened[0:5, :, 0:row_count]
    minus_y = widened[5:10, :, 2 : row_count + 2]
    passed = []
    for dir_index, direction in enumerate(lattice_dirs):
        if dir_index in upward_dirs:
            plane_set = plus_y[upward_dirs.index(dir_index)]
        elif dir_index in downward_dirs:
            plane_set = minus_y[downward_dirs.index(dir_index)]
        else:
            plane_set = along_z[dir_index]
        passed.append(jnp.roll(plane_set, direction[0], axis=2))
    return jnp.stack(passed)


def cubic_table(row_count, coarse, margin, periodic):
    fine_rows = jnp.arange(row_count, dtype=jnp.int32)
    shifted = fine_rows - 2
    base_cell = shifted // 4
    position = ((shifted % 4).astype(jnp.float32) + 0.5) / 4.0
    third_power = position * position * position
    second_power = position * position
    weight_rows = (
        (-third_power + 2.0 * second_power - position) / 2.0,
        (3.0 * third_power - 5.0 * second_power + 2.0) / 2.0,
        (-3.0 * third_power + 4.0 * second_power + position) / 2.0,
        (third_power - second_power) / 2.0,
    )
    columns = jnp.arange(coarse, dtype=jnp.int32)
    interp = jnp.zeros((row_count, coarse), jnp.float32)
    for offset, weight_row in zip((-1, 0, 1, 2), weight_rows):
        target = base_cell + offset + margin
        if periodic:
            target = target % coarse
        interp = interp + weight_row[:, None] * (columns[None, :] == target[:, None]).astype(
            jnp.float32
        )
    return interp


def upsample(scalar_field, x_table, y_table):
    depth_count = scalar_field.shape[0]
    row_count = scalar_field.shape[1]
    col_count = scalar_field.shape[2]
    along_x = jnp.dot(
        scalar_field.reshape(depth_count * row_count, col_count),
        x_table.T,
        precision=lax.Precision.HIGHEST,
        preferred_element_type=jnp.float32,
    )
    along_x = along_x.reshape(depth_count, row_count, x_table.shape[0])
    return jnp.einsum("ry,zyx->zrx", y_table, along_x, precision=lax.Precision.HIGHEST)


def slab_light(sample, total_planes):
    squared = sample * sample
    saturation = squared / (1.0 + squared)
    extinction = optical / total_planes * saturation
    opacity = -jnp.expm1(-extinction)
    optical_depth = jnp.cumsum(extinction, axis=0) - extinction
    weight = jnp.exp(-optical_depth) * opacity
    colors = jnp.stack(
        [saturation, 1.0 / (1.0 + squared), jnp.exp(-0.5 * (sample - 1.0) * (sample - 1.0))]
    )
    radiance = jnp.sum(weight[None] * colors, axis=1)
    depth_total = jnp.sum(extinction, axis=0)
    return (radiance, depth_total)


def body(populations, wall_flags):
    depth_count = populations.shape[1]
    row_count = populations.shape[2]
    col_count = populations.shape[3]
    lattice_state = populations
    for repeat in range(STEPS):
        lattice_state = stream_local(relax(lattice_state, wall_flags))
    scalar_field = speed_gain * moments(lattice_state)[2]
    x_table = cubic_table(4 * col_count, col_count, 0, True)
    coarse_field = with_halo(scalar_field, (("col", 1),), 2)
    y_table = cubic_table(4 * row_count, row_count + 4, 2, False)
    sample = upsample(coarse_field, x_table, y_table)
    slab_count = lax.axis_size("slab")
    radiance, depth_total = slab_light(sample, depth_count * slab_count)
    transmit = jnp.exp(-depth_total)
    ray_rows = radiance.shape[1]
    tile_width = radiance.shape[2] // slab_count
    piece_light = radiance.reshape(3, ray_rows, slab_count, tile_width)
    piece_trans = transmit.reshape(ray_rows, slab_count, tile_width)
    my_slab = lax.axis_index("slab")
    for bit_index in range(slab_count.bit_length() - 1):
        halves = piece_light.shape[2] // 2
        split_light = piece_light.reshape(3, ray_rows, halves, 2, tile_width)
        split_trans = piece_trans.reshape(ray_rows, halves, 2, tile_width)
        is_back = my_slab >> bit_index & 1 == 1
        keep_light = jnp.where(is_back, split_light[:, :, :, 1], split_light[:, :, :, 0])
        send_light = jnp.where(is_back, split_light[:, :, :, 0], split_light[:, :, :, 1])
        keep_trans = jnp.where(is_back, split_trans[:, :, 1], split_trans[:, :, 0])
        send_trans = jnp.where(is_back, split_trans[:, :, 0], split_trans[:, :, 1])
        got_light, got_trans = swapped((send_light, send_trans), "slab", bit_index)
        front_light = jnp.where(is_back, got_light, keep_light)
        back_light = jnp.where(is_back, keep_light, got_light)
        front_trans = jnp.where(is_back, got_trans, keep_trans)
        back_trans = jnp.where(is_back, keep_trans, got_trans)
        piece_light = front_light + front_trans[None] * back_light
        piece_trans = front_trans * back_trans
    image = jnp.concatenate([piece_light[:, :, 0], (1.0 - piece_trans[:, 0])[None]], axis=0)
    return (image, lattice_state)


def solution(mesh):
    return jax.shard_map(
        body,
        mesh=mesh,
        in_specs=(P(None, "slab", "col", None), P("slab", "col", None)),
        out_specs=(P(None, "col", "slab"), P(None, "slab", "col", None)),
        check_vma=False,
    )
```

profile of v0, /device:TPU:54, one launch (start us, length us, event | category | flops | bytes accessed | tf_op | source)
XLA Modules:
  0.0 175.4 jit_solution(10497297779446883901)
XLA Ops:
  5.6 3.1 %collective-permute-start.1 = (f32[19,1,16,128]{3,2,1,0:T(8,128)S(1)}, f32[19,1,16,128]{3,2,1,0:T(8,128)S(1)}, u32[]{:S(2)}, u32[]{:S(2)}) collective-permute-start(f32[19,1,16,128]{3,2,1,0:T(8,128)S(1)} %get-tuple-element.51), channel_id=1, source_target_pairs={{0,2},{2,4},{4,6},{6,8},{8,10},{10,12},{12,14},{14,16},{16,18},{18... | collective-permute-start | bytes 466952 | tf_op jit(solution)/shard_map/ppermute | solution.py:60
  8.7 2.7 %collective-permute-start = (f32[19,1,16,128]{3,2,1,0:T(8,128)S(1)}, f32[19,1,16,128]{3,2,1,0:T(8,128)S(1)}, u32[]{:S(2)}, u32[]{:S(2)}) collective-permute-start(f32[19,1,16,128]{3,2,1,0:T(8,128)S(1)} %get-tuple-element.52), channel_id=1, source_target_pairs={{2,0},{4,2},{6,4},{8,6},{10,8},{12,10},{14,12},{16,14},{18,16},{20... | collective-permute-start | bytes 466952 | tf_op jit(solution)/shard_map/ppermute | solution.py:62
  13.3 4.9 %collective-permute-done = f32[19,1,16,128]{3,2,1,0:T(8,128)S(1)} collective-permute-done((f32[19,1,16,128]{3,2,1,0:T(8,128)S(1)}, f32[19,1,16,128]{3,2,1,0:T(8,128)S(1)}, u32[]{:S(2)}, u32[]{:S(2)}) %collective-permute-start) | collective-permute-done | bytes 155680 | tf_op jit(solution)/shard_map/ppermute | solution.py:62
  20.5 2.4 %collective-permute-start.2 = (f32[10,2,1,128]{3,2,1,0:T(1,128)S(1)}, f32[10,2,1,128]{3,2,1,0:T(1,128)S(1)}, u32[]{:S(2)}, u32[]{:S(2)}) collective-permute-start(f32[10,2,1,128]{3,2,1,0:T(1,128)S(1)} %get-tuple-element.94), channel_id=1, source_target_pairs={{1,0},{0,1},{3,2},{2,3},{5,4},{4,5},{7,6},{6,7},{9,8},{8,9},{11,10... | collective-permute-start | bytes 30728 | tf_op jit(solution)/shard_map/ppermute | solution.py:62
  26.6 1.9 %collective-permute-start.4 = (f32[19,1,16,128]{3,2,1,0:T(8,128)S(1)}, f32[19,1,16,128]{3,2,1,0:T(8,128)S(1)}, u32[]{:S(2)}, u32[]{:S(2)}) collective-permute-start(f32[19,1,16,128]{3,2,1,0:T(8,128)S(1)} %get-tuple-element.46), channel_id=1, source_target_pairs={{0,2},{2,4},{4,6},{6,8},{8,10},{10,12},{12,14},{14,16},{16,18},{18... | collective-permute-start | bytes 466952 | tf_op jit(solution)/shard_map/ppermute | solution.py:60
  28.5 3.9 %collective-permute-start.5 = (f32[19,1,16,128]{3,2,1,0:T(8,128)S(1)}, f32[19,1,16,128]{3,2,1,0:T(8,128)S(1)}, u32[]{:S(2)}, u32[]{:S(2)}) collective-permute-start(f32[19,1,16,128]{3,2,1,0:T(8,128)S(1)} %get-tuple-element.45), channel_id=1, source_target_pairs={{2,0},{4,2},{6,4},{8,6},{10,8},{12,10},{14,12},{16,14},{18,16},{20... | collective-permute-start | bytes 466952 | tf_op jit(solution)/shard_map/ppermute | solution.py:62
  32.4 2.3 %collective-permute-done.4 = f32[19,1,16,128]{3,2,1,0:T(8,128)S(1)} collective-permute-done((f32[19,1,16,128]{3,2,1,0:T(8,128)S(1)}, f32[19,1,16,128]{3,2,1,0:T(8,128)S(1)}, u32[]{:S(2)}, u32[]{:S(2)}) %collective-permute-start.4) | collective-permute-done | bytes 155680 | tf_op jit(solution)/shard_map/ppermute | solution.py:60
  34.7 4.1 %collective-permute-done.5 = f32[19,1,16,128]{3,2,1,0:T(8,128)S(1)} collective-permute-done((f32[19,1,16,128]{3,2,1,0:T(8,128)S(1)}, f32[19,1,16,128]{3,2,1,0:T(8,128)S(1)}, u32[]{:S(2)}, u32[]{:S(2)}) %collective-permute-start.5) | collective-permute-done | bytes 155680 | tf_op jit(solution)/shard_map/ppermute | solution.py:62
  40.8 2.4 %collective-permute-start.6 = (f32[10,2,1,128]{3,2,1,0:T(1,128)S(1)}, f32[10,2,1,128]{3,2,1,0:T(1,128)S(1)}, u32[]{:S(2)}, u32[]{:S(2)}) collective-permute-start(f32[10,2,1,128]{3,2,1,0:T(1,128)S(1)} %get-tuple-element.90), channel_id=1, source_target_pairs={{0,1},{1,0},{2,3},{3,2},{4,5},{5,4},{6,7},{7,6},{8,9},{9,8},{10,11... | collective-permute-start | bytes 30728 | tf_op jit(solution)/shard_map/ppermute | solution.py:60
  46.0 2.2 %collective-permute-start.8 = (f32[2,2,128]{2,1,0:T(2,128)S(1)}, f32[2,2,128]{2,1,0:T(2,128)S(1)}, u32[]{:S(2)}, u32[]{:S(2)}) collective-permute-start(f32[2,2,128]{2,1,0:T(2,128)S(1)} %get-tuple-element.132), channel_id=1, source_target_pairs={{0,1},{1,0},{2,3},{3,2},{4,5},{5,4},{6,7},{7,6},{8,9},{9,8},{10,11... | collective-permute-start | bytes 6152 | tf_op jit(solution)/shard_map/ppermute | solution.py:60
  48.2 2.1 %collective-permute-start.9 = (f32[2,2,128]{2,1,0:T(2,128)S(1)}, f32[2,2,128]{2,1,0:T(2,128)S(1)}, u32[]{:S(2)}, u32[]{:S(2)}) collective-permute-start(f32[2,2,128]{2,1,0:T(2,128)S(1)} %get-tuple-element.133), channel_id=1, source_target_pairs={{1,0},{0,1},{3,2},{2,3},{5,4},{4,5},{7,6},{6,7},{9,8},{8,9},{11,10... | collective-permute-start | bytes 6152 | tf_op jit(solution)/shard_map/ppermute | solution.py:62
  53.1 1.9 %collective-permute-start.11 = (f32[64,128,2]{0,2,1:T(2,128)S(1)}, f32[64,128,2]{0,2,1:T(2,128)S(1)}, u32[]{:S(2)}, u32[]{:S(2)}) collective-permute-start(f32[64,128,2]{0,2,1:T(2,128)S(1)} %fusion.32), channel_id=1, source_target_pairs={{0,2},{2,0},{4,6},{6,4},{8,10},{10,8},{12,14},{14,12},{16,18},{18,... | collective-permute-start | bytes 196616 | tf_op jit(solution)/shard_map/ppermute | solution.py:72
  55.0 5.5 %collective-permute-done.11 = f32[64,128,2]{0,2,1:T(2,128)S(1)} collective-permute-done((f32[64,128,2]{0,2,1:T(2,128)S(1)}, f32[64,128,2]{0,2,1:T(2,128)S(1)}, u32[]{:S(2)}, u32[]{:S(2)}) %collective-permute-start.11) | collective-permute-done | bytes 65568 | tf_op jit(solution)/shard_map/ppermute | solution.py:72
  62.8 5.7 %collective-permute-done.13 = f32[64,64,2]{0,1,2:T(8,128)S(1)} collective-permute-done((f32[64,64,2]{0,1,2:T(8,128)S(1)}, f32[64,64,2]{0,1,2:T(8,128)S(1)}, u32[]{:S(2)}, u32[]{:S(2)}) %collective-permute-start.13) | collective-permute-done | bytes 32800 | tf_op jit(solution)/shard_map/ppermute | solution.py:72
  68.6 7.7 %collective-permute-start.15 = (f32[64,32,2]{0,1,2:T(8,128)S(1)}, f32[64,32,2]{0,1,2:T(8,128)S(1)}, u32[]{:S(2)}, u32[]{:S(2)}) collective-permute-start(f32[64,32,2]{0,1,2:T(8,128)S(1)} %select_bitcast_fusion.4), channel_id=1, source_target_pairs={{0,8},{2,10},{4,12},{6,14},{8,0},{10,2},{12,4},{14,6},{16,24},{18,... | collective-permute-start | bytes 49160 | tf_op jit(solution)/shard_map/ppermute | solution.py:72
  80.5 4.8 %collective-permute-done.17 = f32[64,16,2]{0,1,2:T(8,128)S(1)} collective-permute-done((f32[64,16,2]{0,1,2:T(8,128)S(1)}, f32[64,16,2]{0,1,2:T(8,128)S(1)}, u32[]{:S(2)}, u32[]{:S(2)}) %collective-permute-start.17) | collective-permute-done | bytes 8224 | tf_op jit(solution)/shard_map/ppermute | solution.py:72
  85.4 3.7 %collective-permute-start.19 = (f32[64,8,2]{0,1,2:T(8,128)S(1)}, f32[64,8,2]{0,1,2:T(8,128)S(1)}, u32[]{:S(2)}, u32[]{:S(2)}) collective-permute-start(f32[64,8,2]{0,1,2:T(8,128)S(1)} %select_bitcast_fusion.8), channel_id=1, source_target_pairs={{0,32},{2,34},{4,36},{6,38},{8,40},{10,42},{12,44},{14,46},{16,48}... | collective-permute-start | bytes 12296 | tf_op jit(solution)/shard_map/ppermute | solution.py:72
  89.3 3.0 %collective-permute-start.10 = (f32[3,64,128,2]{1,3,2,0:T(2,128)S(1)}, f32[3,64,128,2]{1,3,2,0:T(2,128)S(1)}, u32[]{:S(2)}, u32[]{:S(2)}) collective-permute-start(f32[3,64,128,2]{1,3,2,0:T(2,128)S(1)} %fusion.8), channel_id=1, source_target_pairs={{0,2},{2,0},{4,6},{6,4},{8,10},{10,8},{12,14},{14,12},{16,18},{18,... | collective-permute-start | bytes 589832 | tf_op jit(solution)/shard_map/ppermute | solution.py:72
  92.4 6.6 %collective-permute-done.10 = f32[3,64,128,2]{1,3,2,0:T(2,128)S(1)} collective-permute-done((f32[3,64,128,2]{1,3,2,0:T(2,128)S(1)}, f32[3,64,128,2]{1,3,2,0:T(2,128)S(1)}, u32[]{:S(2)}, u32[]{:S(2)}) %collective-permute-start.10) | collective-permute-done | bytes 196640 | tf_op jit(solution)/shard_map/ppermute | solution.py:72
  99.8 5.9 %collective-permute-start.12 = (f32[3,64,64,2]{1,2,3,0:T(8,128)S(1)}, f32[3,64,64,2]{1,2,3,0:T(8,128)S(1)}, u32[]{:S(2)}, u32[]{:S(2)}) collective-permute-start(f32[3,64,64,2]{1,2,3,0:T(8,128)S(1)} %select_bitcast_fusion), channel_id=1, source_target_pairs={{0,4},{2,6},{4,0},{6,2},{8,12},{10,14},{12,8},{14,10},{16,20},{18,... | collective-permute-start | bytes 294920 | tf_op jit(solution)/shard_map/ppermute | solution.py:72
  105.7 3.6 %collective-permute-done.12 = f32[3,64,64,2]{1,2,3,0:T(8,128)S(1)} collective-permute-done((f32[3,64,64,2]{1,2,3,0:T(8,128)S(1)}, f32[3,64,64,2]{1,2,3,0:T(8,128)S(1)}, u32[]{:S(2)}, u32[]{:S(2)}) %collective-permute-start.12) | collective-permute-done | bytes 98336 | tf_op jit(solution)/shard_map/ppermute | solution.py:72
  109.5 2.2 %collective-permute-start.14 = (f32[3,64,32,2]{1,2,3,0:T(8,128)S(1)}, f32[3,64,32,2]{1,2,3,0:T(8,128)S(1)}, u32[]{:S(2)}, u32[]{:S(2)}) collective-permute-start(f32[3,64,32,2]{1,2,3,0:T(8,128)S(1)} %select_bitcast_fusion.1), channel_id=1, source_target_pairs={{0,8},{2,10},{4,12},{6,14},{8,0},{10,2},{12,4},{14,6},{16,24},{18,... | collective-permute-start | bytes 147464 | tf_op jit(solution)/shard_map/ppermute | solution.py:72
  111.8 9.5 %collective-permute-start.21 = (f32[64,4,2]{0,1,2:T(4,128)S(1)}, f32[64,4,2]{0,1,2:T(4,128)S(1)}, u32[]{:S(2)}, u32[]{:S(2)}) collective-permute-start(f32[64,4,2]{0,1,2:T(4,128)S(1)} %select_bitcast_fusion.9), channel_id=1, source_target_pairs={{0,64},{2,66},{4,68},{6,70},{8,72},{10,74},{12,76},{14,78},{16,80}... | collective-permute-start | bytes 6152 | tf_op jit(solution)/shard_map/ppermute | solution.py:72
  123.4 5.5 %collective-permute-done.16 = f32[3,64,16,2]{1,2,3,0:T(8,128)S(1)} collective-permute-done((f32[3,64,16,2]{1,2,3,0:T(8,128)S(1)}, f32[3,64,16,2]{1,2,3,0:T(8,128)S(1)}, u32[]{:S(2)}, u32[]{:S(2)}) %collective-permute-start.16) | collective-permute-done | bytes 24608 | tf_op jit(solution)/shard_map/ppermute | solution.py:72
  129.0 4.2 %collective-permute-start.18 = (f32[3,64,8,2]{1,2,3,0:T(8,128)S(1)}, f32[3,64,8,2]{1,2,3,0:T(8,128)S(1)}, u32[]{:S(2)}, u32[]{:S(2)}) collective-permute-start(f32[3,64,8,2]{1,2,3,0:T(8,128)S(1)} %select_bitcast_fusion.5), channel_id=1, source_target_pairs={{0,32},{2,34},{4,36},{6,38},{8,40},{10,42},{12,44},{14,46},{16,48}... | collective-permute-start | bytes 36872 | tf_op jit(solution)/shard_map/ppermute | solution.py:72
  133.2 9.1 %collective-permute-start.23 = (f32[64,2,2]{0,2,1:T(2,128)S(1)}, f32[64,2,2]{0,2,1:T(2,128)S(1)}, u32[]{:S(2)}, u32[]{:S(2)}) collective-permute-start(f32[64,2,2]{0,2,1:T(2,128)S(1)} %fusion.93), channel_id=1, source_target_pairs={{0,128},{2,130},{4,132},{6,134},{8,136},{10,138},{12,140},{14,142}... | collective-permute-start | bytes 3080 | tf_op jit(solution)/shard_map/ppermute | solution.py:72
  142.4 2.5 %collective-permute-start.20 = (f32[3,64,4,2]{1,2,3,0:T(4,128)S(1)}, f32[3,64,4,2]{1,2,3,0:T(4,128)S(1)}, u32[]{:S(2)}, u32[]{:S(2)}) collective-permute-start(f32[3,64,4,2]{1,2,3,0:T(4,128)S(1)} %select_bitcast_fusion.7), channel_id=1, source_target_pairs={{0,64},{2,66},{4,68},{6,70},{8,72},{10,74},{12,76},{14,78},{16,80}... | collective-permute-start | bytes 18440 | tf_op jit(solution)/shard_map/ppermute | solution.py:72
  145.0 3.9 %collective-permute-done.20 = f32[3,64,4,2]{1,2,3,0:T(4,128)S(1)} collective-permute-done((f32[3,64,4,2]{1,2,3,0:T(4,128)S(1)}, f32[3,64,4,2]{1,2,3,0:T(4,128)S(1)}, u32[]{:S(2)}, u32[]{:S(2)}) %collective-permute-start.20) | collective-permute-done | bytes 6176 | tf_op jit(solution)/shard_map/ppermute | solution.py:72
  148.9 2.8 %collective-permute-start.22 = (f32[3,64,2,2]{1,3,2,0:T(2,128)S(1)}, f32[3,64,2,2]{1,3,2,0:T(2,128)S(1)}, u32[]{:S(2)}, u32[]{:S(2)}) collective-permute-start(f32[3,64,2,2]{1,3,2,0:T(2,128)S(1)} %fusion.63), channel_id=1, source_target_pairs={{0,128},{2,130},{4,132},{6,134},{8,136},{10,138},{12,140},{14,142}... | collective-permute-start | bytes 9224 | tf_op jit(solution)/shard_map/ppermute | solution.py:72
  151.8 8.7 %collective-permute-start.25 = (f32[64,1,2]{0,2,1:T(2,128)S(1)}, f32[64,1,2]{0,2,1:T(2,128)S(1)}, u32[]{:S(2)}, u32[]{:S(2)}) collective-permute-start(f32[64,1,2]{0,2,1:T(2,128)S(1)} %select_bitcast_fusion.10), channel_id=1, source_target_pairs={{0,256},{2,258},{4,260},{6,262},{8,264},{10,266},{12,268},{14,270}... | collective-permute-start | bytes 1544 | tf_op jit(solution)/shard_map/ppermute | solution.py:72
  160.6 5.8 %collective-permute-start.24 = (f32[3,64,1,2]{1,3,0,2:T(2,128)S(1)}, f32[3,64,1,2]{1,3,0,2:T(2,128)S(1)}, u32[]{:S(2)}, u32[]{:S(2)}) collective-permute-start(f32[3,64,1,2]{1,3,0,2:T(2,128)S(1)} %fusion.74), channel_id=1, source_target_pairs={{0,256},{2,258},{4,260},{6,262},{8,264},{10,266},{12,268},{14,270}... | collective-permute-start | bytes 4616 | tf_op jit(solution)/shard_map/ppermute | solution.py:72
  166.4 8.3 %collective-permute-done.24 = f32[3,64,1,2]{1,3,0,2:T(2,128)S(1)} collective-permute-done((f32[3,64,1,2]{1,3,0,2:T(2,128)S(1)}, f32[3,64,1,2]{1,3,0,2:T(2,128)S(1)}, u32[]{:S(2)}, u32[]{:S(2)}) %collective-permute-start.24) | collective-permute-done | bytes 1568 | tf_op jit(solution)/shard_map/ppermute | solution.py:72
  (205 shorter events, 30.4 us)
Async XLA Ops:
  1.4 1.1 copy-start
  2.5 0.7 copy-start.1
  3.7 0.7 copy-start.2
  5.6 7.7 %collective-permute-start.1 = (f32[19,1,16,128]{3,2,1,0:T(8,128)S(1)}, f32[19,1,16,128]{3,2,1,0:T(8,128)S(1)}, u32[]{:S(2)}, u32[]{:S(2)}) collective-permute-start(f32[19,1,16,128]{3,2,1,0:T(8,128)S(1)} %get-tuple-element.51), channel_id=1, source_target_pairs={{0,2},{2,4},{4,6},{6,8},{8,10},{10,12},{12,14},{14,16},{16,18},{18... | collective-permute-start | bytes 466952 | tf_op jit(solution)/shard_map/ppermute | solution.py:60
  8.7 9.5 %collective-permute-start = (f32[19,1,16,128]{3,2,1,0:T(8,128)S(1)}, f32[19,1,16,128]{3,2,1,0:T(8,128)S(1)}, u32[]{:S(2)}, u32[]{:S(2)}) collective-permute-start(f32[19,1,16,128]{3,2,1,0:T(8,128)S(1)} %get-tuple-element.52), channel_id=1, source_target_pairs={{2,0},{4,2},{6,4},{8,6},{10,8},{12,10},{14,12},{16,14},{18,16},{20... | collective-permute-start | bytes 466952 | tf_op jit(solution)/shard_map/ppermute | solution.py:62
  18.5 4.7 %collective-permute-start.3 = (f32[10,2,1,128]{3,2,1,0:T(1,128)S(1)}, f32[10,2,1,128]{3,2,1,0:T(1,128)S(1)}, u32[]{:S(2)}, u32[]{:S(2)}) collective-permute-start(f32[10,2,1,128]{3,2,1,0:T(1,128)S(1)} %get-tuple-element.93), channel_id=1, source_target_pairs={{0,1},{1,0},{2,3},{3,2},{4,5},{5,4},{6,7},{7,6},{8,9},{9,8},{10,11... | collective-permute-start | bytes 30728 | tf_op jit(solution)/shard_map/ppermute | solution.py:60
  20.5 3.2 %collective-permute-start.2 = (f32[10,2,1,128]{3,2,1,0:T(1,128)S(1)}, f32[10,2,1,128]{3,2,1,0:T(1,128)S(1)}, u32[]{:S(2)}, u32[]{:S(2)}) collective-permute-start(f32[10,2,1,128]{3,2,1,0:T(1,128)S(1)} %get-tuple-element.94), channel_id=1, source_target_pairs={{1,0},{0,1},{3,2},{2,3},{5,4},{4,5},{7,6},{6,7},{9,8},{8,9},{11,10... | collective-permute-start | bytes 30728 | tf_op jit(solution)/shard_map/ppermute | solution.py:62
  26.6 8.2 %collective-permute-start.4 = (f32[19,1,16,128]{3,2,1,0:T(8,128)S(1)}, f32[19,1,16,128]{3,2,1,0:T(8,128)S(1)}, u32[]{:S(2)}, u32[]{:S(2)}) collective-permute-start(f32[19,1,16,128]{3,2,1,0:T(8,128)S(1)} %get-tuple-element.46), channel_id=1, source_target_pairs={{0,2},{2,4},{4,6},{6,8},{8,10},{10,12},{12,14},{14,16},{16,18},{18... | collective-permute-start | bytes 466952 | tf_op jit(solution)/shard_map/ppermute | solution.py:60
  28.5 10.3 %collective-permute-start.5 = (f32[19,1,16,128]{3,2,1,0:T(8,128)S(1)}, f32[19,1,16,128]{3,2,1,0:T(8,128)S(1)}, u32[]{:S(2)}, u32[]{:S(2)}) collective-permute-start(f32[19,1,16,128]{3,2,1,0:T(8,128)S(1)} %get-tuple-element.45), channel_id=1, source_target_pairs={{2,0},{4,2},{6,4},{8,6},{10,8},{12,10},{14,12},{16,14},{18,16},{20... | collective-permute-start | bytes 466952 | tf_op jit(solution)/shard_map/ppermute | solution.py:62
  38.9 4.8 %collective-permute-start.7 = (f32[10,2,1,128]{3,2,1,0:T(1,128)S(1)}, f32[10,2,1,128]{3,2,1,0:T(1,128)S(1)}, u32[]{:S(2)}, u32[]{:S(2)}) collective-permute-start(f32[10,2,1,128]{3,2,1,0:T(1,128)S(1)} %get-tuple-element.89), channel_id=1, source_target_pairs={{1,0},{0,1},{3,2},{2,3},{5,4},{4,5},{7,6},{6,7},{9,8},{8,9},{11,10... | collective-permute-start | bytes 30728 | tf_op jit(solution)/shard_map/ppermute | solution.py:62
  40.8 3.2 %collective-permute-start.6 = (f32[10,2,1,128]{3,2,1,0:T(1,128)S(1)}, f32[10,2,1,128]{3,2,1,0:T(1,128)S(1)}, u32[]{:S(2)}, u32[]{:S(2)}) collective-permute-start(f32[10,2,1,128]{3,2,1,0:T(1,128)S(1)} %get-tuple-element.90), channel_id=1, source_target_pairs={{0,1},{1,0},{2,3},{3,2},{4,5},{5,4},{6,7},{7,6},{8,9},{9,8},{10,11... | collective-permute-start | bytes 30728 | tf_op jit(solution)/shard_map/ppermute | solution.py:60
  45.3 0.7 copy-start.3
  46.0 4.4 %collective-permute-start.8 = (f32[2,2,128]{2,1,0:T(2,128)S(1)}, f32[2,2,128]{2,1,0:T(2,128)S(1)}, u32[]{:S(2)}, u32[]{:S(2)}) collective-permute-start(f32[2,2,128]{2,1,0:T(2,128)S(1)} %get-tuple-element.132), channel_id=1, source_target_pairs={{0,1},{1,0},{2,3},{3,2},{4,5},{5,4},{6,7},{7,6},{8,9},{9,8},{10,11... | collective-permute-start | bytes 6152 | tf_op jit(solution)/shard_map/ppermute | solution.py:60
  48.2 3.1 %collective-permute-start.9 = (f32[2,2,128]{2,1,0:T(2,128)S(1)}, f32[2,2,128]{2,1,0:T(2,128)S(1)}, u32[]{:S(2)}, u32[]{:S(2)}) collective-permute-start(f32[2,2,128]{2,1,0:T(2,128)S(1)} %get-tuple-element.133), channel_id=1, source_target_pairs={{1,0},{0,1},{3,2},{2,3},{5,4},{4,5},{7,6},{6,7},{9,8},{8,9},{11,10... | collective-permute-start | bytes 6152 | tf_op jit(solution)/shard_map/ppermute | solution.py:62
  53.1 7.5 %collective-permute-start.11 = (f32[64,128,2]{0,2,1:T(2,128)S(1)}, f32[64,128,2]{0,2,1:T(2,128)S(1)}, u32[]{:S(2)}, u32[]{:S(2)}) collective-permute-start(f32[64,128,2]{0,2,1:T(2,128)S(1)} %fusion.32), channel_id=1, source_target_pairs={{0,2},{2,0},{4,6},{6,4},{8,10},{10,8},{12,14},{14,12},{16,18},{18,... | collective-permute-start | bytes 196616 | tf_op jit(solution)/shard_map/ppermute | solution.py:72
  60.8 7.7 %collective-permute-start.13 = (f32[64,64,2]{0,1,2:T(8,128)S(1)}, f32[64,64,2]{0,1,2:T(8,128)S(1)}, u32[]{:S(2)}, u32[]{:S(2)}) collective-permute-start(f32[64,64,2]{0,1,2:T(8,128)S(1)} %select_bitcast_fusion.2), channel_id=1, source_target_pairs={{0,4},{2,6},{4,0},{6,2},{8,12},{10,14},{12,8},{14,10},{16,20},{18,... | collective-permute-start | bytes 98312 | tf_op jit(solution)/shard_map/ppermute | solution.py:72
  68.6 9.6 %collective-permute-start.15 = (f32[64,32,2]{0,1,2:T(8,128)S(1)}, f32[64,32,2]{0,1,2:T(8,128)S(1)}, u32[]{:S(2)}, u32[]{:S(2)}) collective-permute-start(f32[64,32,2]{0,1,2:T(8,128)S(1)} %select_bitcast_fusion.4), channel_id=1, source_target_pairs={{0,8},{2,10},{4,12},{6,14},{8,0},{10,2},{12,4},{14,6},{16,24},{18,... | collective-permute-start | bytes 49160 | tf_op jit(solution)/shard_map/ppermute | solution.py:72
  78.2 7.1 %collective-permute-start.17 = (f32[64,16,2]{0,1,2:T(8,128)S(1)}, f32[64,16,2]{0,1,2:T(8,128)S(1)}, u32[]{:S(2)}, u32[]{:S(2)}) collective-permute-start(f32[64,16,2]{0,1,2:T(8,128)S(1)} %select_bitcast_fusion.6), channel_id=1, source_target_pairs={{0,16},{2,18},{4,20},{6,22},{8,24},{10,26},{12,28},{14,30},{16,0},... | collective-permute-start | bytes 24584 | tf_op jit(solution)/shard_map/ppermute | solution.py:72
  85.4 7.0 %collective-permute-start.19 = (f32[64,8,2]{0,1,2:T(8,128)S(1)}, f32[64,8,2]{0,1,2:T(8,128)S(1)}, u32[]{:S(2)}, u32[]{:S(2)}) collective-permute-start(f32[64,8,2]{0,1,2:T(8,128)S(1)} %select_bitcast_fusion.8), channel_id=1, source_target_pairs={{0,32},{2,34},{4,36},{6,38},{8,40},{10,42},{12,44},{14,46},{16,48}... | collective-permute-start | bytes 12296 | tf_op jit(solution)/shard_map/ppermute | solution.py:72
  89.3 9.7 %collective-permute-start.10 = (f32[3,64,128,2]{1,3,2,0:T(2,128)S(1)}, f32[3,64,128,2]{1,3,2,0:T(2,128)S(1)}, u32[]{:S(2)}, u32[]{:S(2)}) collective-permute-start(f32[3,64,128,2]{1,3,2,0:T(2,128)S(1)} %fusion.8), channel_id=1, source_target_pairs={{0,2},{2,0},{4,6},{6,4},{8,10},{10,8},{12,14},{14,12},{16,18},{18,... | collective-permute-start | bytes 589832 | tf_op jit(solution)/shard_map/ppermute | solution.py:72
  99.8 9.5 %collective-permute-start.12 = (f32[3,64,64,2]{1,2,3,0:T(8,128)S(1)}, f32[3,64,64,2]{1,2,3,0:T(8,128)S(1)}, u32[]{:S(2)}, u32[]{:S(2)}) collective-permute-start(f32[3,64,64,2]{1,2,3,0:T(8,128)S(1)} %select_bitcast_fusion), channel_id=1, source_target_pairs={{0,4},{2,6},{4,0},{6,2},{8,12},{10,14},{12,8},{14,10},{16,20},{18,... | collective-permute-start | bytes 294920 | tf_op jit(solution)/shard_map/ppermute | solution.py:72
  109.5 11.7 %collective-permute-start.14 = (f32[3,64,32,2]{1,2,3,0:T(8,128)S(1)}, f32[3,64,32,2]{1,2,3,0:T(8,128)S(1)}, u32[]{:S(2)}, u32[]{:S(2)}) collective-permute-start(f32[3,64,32,2]{1,2,3,0:T(8,128)S(1)} %select_bitcast_fusion.1), channel_id=1, source_target_pairs={{0,8},{2,10},{4,12},{6,14},{8,0},{10,2},{12,4},{14,6},{16,24},{18,... | collective-permute-start | bytes 147464 | tf_op jit(solution)/shard_map/ppermute | solution.py:72
  111.8 11.6 %collective-permute-start.21 = (f32[64,4,2]{0,1,2:T(4,128)S(1)}, f32[64,4,2]{0,1,2:T(4,128)S(1)}, u32[]{:S(2)}, u32[]{:S(2)}) collective-permute-start(f32[64,4,2]{0,1,2:T(4,128)S(1)} %select_bitcast_fusion.9), channel_id=1, source_target_pairs={{0,64},{2,66},{4,68},{6,70},{8,72},{10,74},{12,76},{14,78},{16,80}... | collective-permute-start | bytes 6152 | tf_op jit(solution)/shard_map/ppermute | solution.py:72
  121.4 7.5 %collective-permute-start.16 = (f32[3,64,16,2]{1,2,3,0:T(8,128)S(1)}, f32[3,64,16,2]{1,2,3,0:T(8,128)S(1)}, u32[]{:S(2)}, u32[]{:S(2)}) collective-permute-start(f32[3,64,16,2]{1,2,3,0:T(8,128)S(1)} %select_bitcast_fusion.3), channel_id=1, source_target_pairs={{0,16},{2,18},{4,20},{6,22},{8,24},{10,26},{12,28},{14,30},{16,0},... | collective-permute-start | bytes 73736 | tf_op jit(solution)/shard_map/ppermute | solution.py:72
  129.0 13.3 %collective-permute-start.18 = (f32[3,64,8,2]{1,2,3,0:T(8,128)S(1)}, f32[3,64,8,2]{1,2,3,0:T(8,128)S(1)}, u32[]{:S(2)}, u32[]{:S(2)}) collective-permute-start(f32[3,64,8,2]{1,2,3,0:T(8,128)S(1)} %select_bitcast_fusion.5), channel_id=1, source_target_pairs={{0,32},{2,34},{4,36},{6,38},{8,40},{10,42},{12,44},{14,46},{16,48}... | collective-permute-start | bytes 36872 | tf_op jit(solution)/shard_map/ppermute | solution.py:72
  133.2 11.7 %collective-permute-start.23 = (f32[64,2,2]{0,2,1:T(2,128)S(1)}, f32[64,2,2]{0,2,1:T(2,128)S(1)}, u32[]{:S(2)}, u32[]{:S(2)}) collective-permute-start(f32[64,2,2]{0,2,1:T(2,128)S(1)} %fusion.93), channel_id=1, source_target_pairs={{0,128},{2,130},{4,132},{6,134},{8,136},{10,138},{12,140},{14,142}... | collective-permute-start | bytes 3080 | tf_op jit(solution)/shard_map/ppermute | solution.py:72
  142.4 6.5 %collective-permute-start.20 = (f32[3,64,4,2]{1,2,3,0:T(4,128)S(1)}, f32[3,64,4,2]{1,2,3,0:T(4,128)S(1)}, u32[]{:S(2)}, u32[]{:S(2)}) collective-permute-start(f32[3,64,4,2]{1,2,3,0:T(4,128)S(1)} %select_bitcast_fusion.7), channel_id=1, source_target_pairs={{0,64},{2,66},{4,68},{6,70},{8,72},{10,74},{12,76},{14,78},{16,80}... | collective-permute-start | bytes 18440 | tf_op jit(solution)/shard_map/ppermute | solution.py:72
  148.9 11.6 %collective-permute-start.22 = (f32[3,64,2,2]{1,3,2,0:T(2,128)S(1)}, f32[3,64,2,2]{1,3,2,0:T(2,128)S(1)}, u32[]{:S(2)}, u32[]{:S(2)}) collective-permute-start(f32[3,64,2,2]{1,3,2,0:T(2,128)S(1)} %fusion.63), channel_id=1, source_target_pairs={{0,128},{2,130},{4,132},{6,134},{8,136},{10,138},{12,140},{14,142}... | collective-permute-start | bytes 9224 | tf_op jit(solution)/shard_map/ppermute | solution.py:72
  151.8 14.6 %collective-permute-start.25 = (f32[64,1,2]{0,2,1:T(2,128)S(1)}, f32[64,1,2]{0,2,1:T(2,128)S(1)}, u32[]{:S(2)}, u32[]{:S(2)}) collective-permute-start(f32[64,1,2]{0,2,1:T(2,128)S(1)} %select_bitcast_fusion.10), channel_id=1, source_target_pairs={{0,256},{2,258},{4,260},{6,262},{8,264},{10,266},{12,268},{14,270}... | collective-permute-start | bytes 1544 | tf_op jit(solution)/shard_map/ppermute | solution.py:72
  160.6 14.2 %collective-permute-start.24 = (f32[3,64,1,2]{1,3,0,2:T(2,128)S(1)}, f32[3,64,1,2]{1,3,0,2:T(2,128)S(1)}, u32[]{:S(2)}, u32[]{:S(2)}) collective-permute-start(f32[3,64,1,2]{1,3,0,2:T(2,128)S(1)} %fusion.74), channel_id=1, source_target_pairs={{0,256},{2,258},{4,260},{6,262},{8,264},{10,266},{12,268},{14,270}... | collective-permute-start | bytes 4616 | tf_op jit(solution)/shard_map/ppermute | solution.py:72
where the time goes:
time: 176 us; the launch traced here: 175 us
  starting transfers between devices  97.6 us (55%)
  waiting for transfers between devices  60.2 us (34%)
  other arithmetic  7.1 us (4%)
  local copies, waits for them, and re-layouts  4.72 us (3%)
  matrix products  4.11 us (2%)
    ppermute x16, starting transfers between devices, swapped(): return lax.ppermute(value, axis, pairs)  72.9 us
    ppermute x16, waiting for transfers between devices, swapped(): return lax.ppermute(value, axis, pairs)  45.6 us
    ppermute x5, starting transfers between devices, with_halo(): lax.ppermute(head, axis, [((i + 1) % count, i) for i in range(count)])  13.1 us
    ppermute x5, starting transfers between devices, with_halo(): lax.ppermute(tail, axis, [(i, (i + 1) % count) for i in range(count)])  11.6 us
    ppermute x5, waiting for transfers between devices, with_halo(): lax.ppermute(head, axis, [((i + 1) % count, i) for i in range(count)])  10.3 us
    ppermute x5, waiting for transfers between devices, with_halo(): lax.ppermute(tail, axis, [(i, (i + 1) % count) for i in range(count)])  4.25 us
  transfers between devices with their start and end apart: 26, of which 16 were waited for; matrix products, arithmetic and copies ran while one was open for 1% of the time, Pallas kernels for 0%

commit v1 on v0

v1 whole, which is shorter than its diff:
```python
import functools

import jax
import jax.numpy as jnp
import numpy as np
from jax import lax
from jax.experimental import pallas as pl
from jax.experimental.pallas import tpu as pltpu
from jax.sharding import PartitionSpec as P

DIRS = (
    (0, 0, 0),
    (0, 0, 1), (1, 0, 1), (-1, 0, 1), (0, 1, 1), (0, -1, 1),
    (0, 0, -1), (1, 0, -1), (-1, 0, -1), (0, 1, -1), (0, -1, -1),
    (1, 0, 0), (-1, 0, 0), (0, 1, 0), (0, -1, 0),
    (1, 1, 0), (-1, -1, 0), (1, -1, 0), (-1, 1, 0),
)
OPP = tuple(DIRS.index(tuple(-e for e in d)) for d in DIRS)
WEIGHTS = tuple((1.0 / 3.0, 1.0 / 18.0, 1.0 / 36.0)[sum(abs(e) for e in d)] for d in DIRS)
UP = tuple(i for i, d in enumerate(DIRS) if d[2] == 1)
MID = tuple(i for i, d in enumerate(DIRS) if d[2] == 0)
DOWN = tuple(i for i, d in enumerate(DIRS) if d[2] == -1)
SPEED_GAIN = 10000.0
OPTICAL = 2.0

FLAG = len(MID) + 2 * len(UP)
UNITS = FLAG + 1
UP_SLOT = {d: k for k, d in enumerate(MID + UP)}
UP_FAR = {d: len(MID) + len(UP) + k for k, d in enumerate(UP)}
DOWN_SLOT = {d: k for k, d in enumerate(MID + DOWN)}
DOWN_FAR = {d: len(MID) + len(DOWN) + k for k, d in enumerate(DOWN)}

VMEM_BYTES = 12 << 20
HALO = 4


def along(direction, vector):
    total = None
    for element, part in zip(direction, vector):
        if element:
            term = part if element > 0 else -part
            total = term if total is None else total + term
    return total


def add_moments(state):
    density = state[0]
    momentum = [None, None, None]
    for i in range(1, len(DIRS)):
        density = density + state[i]
        for axis, element in enumerate(DIRS[i]):
            if element:
                held = momentum[axis]
                if held is None:
                    momentum[axis] = state[i] if element > 0 else -state[i]
                else:
                    momentum[axis] = held + state[i] if element > 0 else held - state[i]
    return density, momentum


def relax(state, wall, wanted):
    density, momentum = add_moments(state)
    inverse = 1.0 / density
    velocity = [part * inverse for part in momentum]
    speed_sq = velocity[0] * velocity[0] + velocity[1] * velocity[1] + velocity[2] * velocity[2]
    rest = 1.0 - 1.5 * speed_sq
    scaled = {w: w * density for w in set(WEIGHTS)}
    out = {}
    for i, direction in enumerate(DIRS):
        if i > OPP[i] or (i not in wanted and OPP[i] not in wanted):
            continue
        mass = scaled[WEIGHTS[i]]
        if i == 0:
            out[0] = jnp.where(wall, state[0], mass * rest)
            continue
        project = along(direction, velocity)
        even = rest + 4.5 * project * project
        odd = 3.0 * project
        if i in wanted:
            out[i] = jnp.where(wall, state[OPP[i]], mass * (even + odd))
        if OPP[i] in wanted:
            out[OPP[i]] = jnp.where(wall, state[i], mass * (even - odd))
    return out


def edge_kernel(pops_ref, flags_ref, edge_ref):
    lower = lax.broadcasted_iota(jnp.int32, (8, 128), 0) < HALO
    for plane in range(2):
        for i in range(len(DIRS)):
            edge_ref[i, plane] = jnp.where(lower, pops_ref[i, plane, 0:8], pops_ref[i, plane, 8:16])
        flags = jnp.where(lower, flags_ref[plane, 0:8], flags_ref[plane, 8:16])
        edge_ref[len(DIRS), plane] = flags.astype(jnp.float32)


def first_kernel(pops_ref, flags_ref, edge_ref, up_ref, down_ref):
    for plane in range(2):
        for tile in range(3):
            rows = slice(8 * tile, 8 * tile + 8)
            if tile < 2:
                state = [pops_ref[i, plane, rows] for i in range(len(DIRS))]
                flags = flags_ref[plane, rows].astype(jnp.float32)
            else:
                state = [edge_ref[i, plane] for i in range(len(DIRS))]
                flags = edge_ref[len(DIRS), plane]
            out = relax(state, flags > 0.5, range(len(DIRS)))
            near, far_slot, near_slot, far_ref, far_dirs = (
                (down_ref, UP_FAR, DOWN_SLOT, up_ref, UP)
                if plane == 0
                else (up_ref, DOWN_FAR, UP_SLOT, down_ref, DOWN)
            )
            for i, slot in near_slot.items():
                near[slot, rows] = out[i]
            for i in far_dirs:
                far_ref[far_slot[i], rows] = out[i]
            near[FLAG, rows] = flags


def shifted(value, direction):
    cx, cy, _ = direction
    if cy:
        value = pltpu.roll(value, cy % value.shape[0], 0)
    if cx:
        value = pltpu.roll(value, cx % value.shape[1], 1)
    return value


def second_kernel(up_ref, down_ref, below_ref, above_ref, table_ref, final_ref, send_ref, passed_ref, relaxed_ref, spread_ref):
    near = ((below_ref, UP_SLOT), (down_ref, DOWN_SLOT), (up_ref, UP_SLOT), (above_ref, DOWN_SLOT))
    from_below = ((below_ref, UP_FAR), (below_ref, UP_SLOT), (up_ref, UP_FAR), (up_ref, UP_SLOT))
    from_above = ((down_ref, DOWN_SLOT), (down_ref, DOWN_FAR), (above_ref, DOWN_SLOT), (above_ref, DOWN_FAR))
    wanted = (UP, range(len(DIRS)), range(len(DIRS)), DOWN)
    spread_ref[...] = jnp.zeros(spread_ref.shape, jnp.float32)
    for plane in range(4):
        for i, direction in enumerate(DIRS):
            ref, slots = (near, from_below, from_above)[direction[2]][plane]
            passed_ref[plane, i] = shifted(ref[slots[i]], direction)
        for tile in range(3):
            rows = slice(8 * tile, 8 * tile + 8)
            state = [passed_ref[plane, i, rows] for i in range(len(DIRS))]
            out = relax(state, near[plane][0][FLAG, rows] > 0.5, wanted[plane])
            for i in wanted[plane]:
                relaxed_ref[plane, i, rows] = out[i]
    for plane in range(2):
        state = []
        for i, direction in enumerate(DIRS):
            value = shifted(relaxed_ref[plane + 1 - direction[2], i], direction)
            final_ref[i, plane] = value[0:16]
            state.append(value)
        density, momentum = add_moments(state)
        inverse = 1.0 / density
        velocity = [part * inverse for part in momentum]
        scalar = SPEED_GAIN * (velocity[0] * velocity[0] + velocity[1] * velocity[1] + velocity[2] * velocity[2])
        spread_ref[24 * plane : 24 * plane + 24, 0:128] = scalar
        spread_ref[64 + 24 * plane : 64 + 24 * plane + 24, 128:256] = scalar
    send_ref[...] = lax.dot_general(
        table_ref[...],
        spread_ref[...],
        (((1,), (1,)), ((), ())),
        precision=lax.Precision.HIGHEST,
        preferred_element_type=jnp.float32,
    )


def render_kernel(total_planes, got_ref, table_ref, image_ref):
    slabs = got_ref.shape[0]
    groups = slabs // 8
    ordered = jnp.concatenate([got_ref[pl.ds(j, 8, stride=groups), :] for j in range(groups)], axis=0)
    samples = jnp.dot(
        ordered, table_ref[...], precision=lax.Precision.HIGHEST, preferred_element_type=jnp.float32
    )
    depth = jnp.zeros((8, 128), jnp.float32)
    light = [jnp.zeros((8, 128), jnp.float32) for _ in range(3)]
    for j in range(groups):
        for plane in range(2):
            sample = samples[8 * j : 8 * j + 8, 128 * plane : 128 * plane + 128]
            squared = sample * sample
            green = 1.0 / (1.0 + squared)
            saturation = squared * green
            extinction = (OPTICAL / total_planes) * saturation
            opacity = extinction * (
                1.0 - extinction * (0.5 - extinction * (1.0 / 6.0 - extinction * (1.0 / 24.0)))
            )
            blue = jnp.exp(-0.5 * (sample - 1.0) * (sample - 1.0))
            weight = jnp.exp(-depth) * opacity
            light[0] = light[0] + weight * saturation
            light[1] = light[1] + weight * green
            light[2] = light[2] + weight * blue
            depth = depth + extinction
    row = lax.broadcasted_iota(jnp.int32, (8, 128), 0)
    ahead = depth
    for step in (1, 2, 4):
        ahead = ahead + jnp.where(row >= step, pltpu.roll(ahead, step, 0), 0.0)
    through = jnp.exp(depth - ahead)
    sums = [jnp.sum(part * through, axis=0, keepdims=True) for part in light]
    sums.append(1.0 - jnp.exp(-jnp.sum(depth, axis=0, keepdims=True)))
    for channel, value in enumerate(sums):
        image_ref[channel, 0:1, :] = value[:, 0:64]
        image_ref[channel, 1:2, :] = value[:, 64:128]


def cubic_weights(row):
    t = (row % 4 + 0.5) / 4.0
    return (
        (-(t**3) + 2.0 * t**2 - t) / 2.0,
        (3.0 * t**3 - 5.0 * t**2 + 2.0) / 2.0,
        (-3.0 * t**3 + 4.0 * t**2 + t) / 2.0,
        (t**3 - t**2) / 2.0,
    )


def x_table(nodes):
    table = np.zeros((2 * nodes, 2 * nodes), np.float32)
    for fine in range(4 * nodes):
        for offset, weight in zip((-1, 0, 1, 2), cubic_weights(fine - 2)):
            table[fine // 2, (fine % 2) * nodes + ((fine - 2) // 4 + offset) % nodes] += weight
    return table


def y_table(rows):
    held = rows + 2 * HALO
    table = np.zeros((128, 256), np.float32)
    for fine in range(4 * rows):
        for offset, weight in zip((-1, 0, 1, 2), cubic_weights(fine - 2)):
            for column in range(2):
                for plane in range(2):
                    source = 64 * column + held * plane + ((fine - 2) // 4 + offset) % held
                    table[source, 128 * plane + 4 * rows * column + fine] += weight
    return table


def call(kernel, outs, scratch=(), name=None):
    vmem = pl.BlockSpec(memory_space=pltpu.VMEM)

    def run(*operands):
        shapes = [jax.ShapeDtypeStruct(shape, jnp.float32) for shape in outs]
        return pl.pallas_call(
            kernel,
            out_shape=shapes,
            in_specs=[vmem] * len(operands),
            out_specs=[vmem] * len(outs),
            scratch_shapes=[pltpu.VMEM(shape, jnp.float32) for shape in scratch],
            compiler_params=pltpu.CompilerParams(vmem_limit_bytes=VMEM_BYTES),
            name=name,
        )(*operands)

    return run


def body(populations, wall_flags):
    slabs = lax.axis_size("slab")
    dirs, planes, rows, nodes = populations.shape
    held = rows + 2 * HALO
    (edge,) = call(edge_kernel, [(dirs + 1, planes, 8, nodes)], name="edge")(populations, wall_flags)
    edge = lax.ppermute(edge, "col", [(0, 1), (1, 0)])
    message = (UNITS, held, nodes)
    up, down = call(first_kernel, [message, message], name="first")(populations, wall_flags, edge)
    below = lax.ppermute(up, "slab", [(i, (i + 1) % slabs) for i in range(slabs)])
    above = lax.ppermute(down, "slab", [((i + 1) % slabs, i) for i in range(slabs)])
    final, send = call(
        second_kernel,
        [populations.shape, (slabs, 128)],
        scratch=[(4, dirs, held, nodes), (4, dirs, held, nodes), (128, 256)],
        name="second",
    )(up, down, below, above, jnp.asarray(x_table(nodes)))
    got = lax.all_to_all(send, "slab", 0, 0, tiled=True)
    (image,) = call(
        functools.partial(render_kernel, planes * slabs), [(4, 2, 4 * rows)], name="render"
    )(got, jnp.asarray(y_table(rows)))
    return jnp.transpose(image, (0, 2, 1)), final


def solution(mesh):
    return jax.shard_map(
        body,
        mesh=mesh,
        in_specs=(P(None, "slab", "col", None), P("slab", "col", None)),
        out_specs=(P(None, "col", "slab"), P(None, "slab", "col", None)),
        check_vma=False,
    )
```

time: 176 us -> 66.1 us (0.38)
  the two profiles are of different devices: /device:TPU:54 before, /device:TPU:2 now
where the time goes in v1:
time: 66.1 us; the launch traced here: 65.8 us
  blocking collectives  42.1 us (64%)
  starting transfers between devices  11.8 us (18%)
  waiting for transfers between devices  6.86 us (10%)
  Pallas kernels  2.64 us (4%)
  local copies, waits for them, and re-layouts  1.69 us (3%)
  between operations  0.68 us (1%)
    all_to_all x1, blocking collectives, body(): got = lax.all_to_all(send, 'slab', 0, 0, tiled=True)  42.1 us
    ppermute x1, starting transfers between devices, body(): lax.ppermute(down, 'slab', [((i + 1) % slabs, i) for i in range(slabs)])  6.31 us
    ppermute x1, waiting for transfers between devices, body(): lax.ppermute(up, 'slab', [(i, (i + 1) % slabs) for i in range(slabs)])  4.32 us
    ppermute x1, starting transfers between devices, body(): lax.ppermute(up, 'slab', [(i, (i + 1) % slabs) for i in range(slabs)])  3.4 us
    pallas_call x4, Pallas kernels, run(): pl.pallas_call(kernel, out_shape=shapes, in_specs=[vmem] * len(operands),...  2.64 us
    ppermute x1, starting transfers between devices, body(): edge = lax.ppermute(edge, 'col', [(0, 1), (1, 0)])  2.05 us
    unnamed x8, local copies, waits for them, and re-layouts  1.69 us
    ppermute x1, waiting for transfers between devices, body(): edge = lax.ppermute(edge, 'col', [(0, 1), (1, 0)])  1.36 us
  transfers between devices with their start and end apart: 3, of which 3 were waited for; matrix products, arithmetic and copies ran while one was open for 0% of the time, Pallas kernels for 0%

profile of v1, /device:TPU:2, one launch (start us, length us, event | category | flops | bytes accessed | tf_op | source)
XLA Modules:
  0.0 65.8 jit_solution(8951164267084932270)
XLA Ops:
  0.6 0.0 copy-start
  0.6 1.0 %copy-done = f32[19,2,16,128]{3,2,1,0:T(8,128)S(1)} copy-done((f32[19,2,16,128]{3,2,1,0:T(8,128)S(1)}, f32[19,2,16,128]{3,2,1,0:T(8,128)}, u32[]{:S(2)}) %copy-start) | copy-done | bytes 311320
  1.6 0.0 copy-start.3
  1.6 0.7 %copy-done.3 = s32[2,16,128]{2,1,0:T(8,128)S(1)} copy-done((s32[2,16,128]{2,1,0:T(8,128)S(1)}, s32[2,16,128]{2,1,0:T(8,128)}, u32[]{:S(2)}) %copy-start.3) | copy-done | bytes 16408
  2.3 0.0 copy-start.1
  2.4 2.1 %collective-permute-start = (f32[20,2,8,128]{3,2,1,0:T(8,128)S(1)}, f32[20,2,8,128]{3,2,1,0:T(8,128)S(1)}, u32[]{:S(2)}, u32[]{:S(2)}) collective-permute-start(f32[20,2,8,128]{3,2,1,0:T(8,128)S(1)} %edge.1), channel_id=1, source_target_pairs={{0,1},{1,0},{2,3},{3,2},{4,5},{5,4},{6,7},{7,6},{8,9},{9,8},{10,11... | collective-permute-start | bytes 491528 | tf_op jit(solution)/shard_map/ppermute | solution.py:254
  4.4 1.4 %collective-permute-done.edge_ref = f32[20,2,8,128]{3,2,1,0:T(8,128)S(1)} collective-permute-done((f32[20,2,8,128]{3,2,1,0:T(8,128)S(1)}, f32[20,2,8,128]{3,2,1,0:T(8,128)S(1)}, u32[]{:S(2)}, u32[]{:S(2)}) %collective-permute-start) | collective-permute-done | bytes 163872 | tf_op jit(solution)/shard_map/ppermute | solution.py:254
  5.8 0.2 first.1
  5.9 3.4 %collective-permute-start.1 = (f32[20,24,128]{2,1,0:T(8,128)S(1)}, f32[20,24,128]{2,1,0:T(8,128)S(1)}, u32[]{:S(2)}, u32[]{:S(2)}) collective-permute-start(f32[20,24,128]{2,1,0:T(8,128)S(1)} %get-tuple-element.6.up_ref), channel_id=1, source_target_pairs={{0,2},{2,4},{4,6},{6,8},{8,10},{10,12},{12,14},{14,16},{16,18},{18... | collective-permute-start | bytes 737288 | tf_op jit(solution)/shard_map/ppermute | solution.py:257
  9.3 6.3 %collective-permute-start.2 = (f32[20,24,128]{2,1,0:T(8,128)S(1)}, f32[20,24,128]{2,1,0:T(8,128)S(1)}, u32[]{:S(2)}, u32[]{:S(2)}) collective-permute-start(f32[20,24,128]{2,1,0:T(8,128)S(1)} %get-tuple-element.7.down_ref), channel_id=1, source_target_pairs={{2,0},{4,2},{6,4},{8,6},{10,8},{12,10},{14,12},{16,14},{18,16},{20... | collective-permute-start | bytes 737288 | tf_op jit(solution)/shard_map/ppermute | solution.py:258
  15.7 4.3 %collective-permute-done.1.below_ref = f32[20,24,128]{2,1,0:T(8,128)S(1)} collective-permute-done((f32[20,24,128]{2,1,0:T(8,128)S(1)}, f32[20,24,128]{2,1,0:T(8,128)S(1)}, u32[]{:S(2)}, u32[]{:S(2)}) %collective-permute-start.1) | collective-permute-done | bytes 245792 | tf_op jit(solution)/shard_map/ppermute | solution.py:257
  20.0 1.2 %collective-permute-done.2.above_ref = f32[20,24,128]{2,1,0:T(8,128)S(1)} collective-permute-done((f32[20,24,128]{2,1,0:T(8,128)S(1)}, f32[20,24,128]{2,1,0:T(8,128)S(1)}, u32[]{:S(2)}, u32[]{:S(2)}) %collective-permute-start.2) | collective-permute-done | bytes 245792 | tf_op jit(solution)/shard_map/ppermute | solution.py:258
  21.2 0.0 copy-done.1
  21.2 1.2 %second.1 = (f32[19,2,16,128]{3,2,1,0:T(8,128)}, f32[256,128]{1,0:T(8,128)S(1)}) custom-call(f32[20,24,128]{2,1,0:T(8,128)S(1)} %get-tuple-element.6.up_ref, f32[20,24,128]{2,1,0:T(8,128)S(1)} %get-tuple-element.7.down_ref, f32[20,24,128]{2,1,0:T(8,128)S(1)} %collective-permute-done.1.below_ref, f32[20,24,128]{2,1,0:T(8,128)S(1)} %collective-permute-done.2.above_ref, ...), custom_call_target="tpu_custom_call" | custom-call | tf_op jit(solution)/shard_map/second/pallas_call | solution.py:236
  22.4 0.0 copy-start.2
  22.4 42.1 %all_to_all.11 = f32[256,1,128]{2,1,0:T(1,128)S(1)} all-to-all(f32[256,1,128]{2,1,0:T(1,128)S(1)} %bitcast.6), channel_id=1, replica_groups=mesh['slab'=256,'col'=2] {'slab'}, dimensions={0} | all-to-all | bytes 262144 | tf_op jit(solution)/shard_map/all_to_all | solution.py:265
  64.5 0.0 copy-done.2
  64.5 1.2 %render.1 = f32[4,2,64]{2,1,0:T(2,128)} custom-call(f32[256,128]{1,0:T(8,128)S(1)} %bitcast.5, f32[128,256]{1,0:T(8,128)S(1)} %copy-done.2), custom_call_target="tpu_custom_call" | custom-call | tf_op jit(solution)/shard_map/render/pallas_call | solution.py:236
  (1 shorter events, 0.0 us)
Async XLA Ops:
  0.6 1.0 %copy-start = (f32[19,2,16,128]{3,2,1,0:T(8,128)S(1)}, f32[19,2,16,128]{3,2,1,0:T(8,128)}, u32[]{:S(2)}) copy-start(f32[19,2,16,128]{3,2,1,0:T(8,128)} %pops_ref.3) | copy-start | bytes 933892
  1.6 0.7 %copy-start.3 = (s32[2,16,128]{2,1,0:T(8,128)S(1)}, s32[2,16,128]{2,1,0:T(8,128)}, u32[]{:S(2)}) copy-start(s32[2,16,128]{2,1,0:T(8,128)} %flags_ref.3) | copy-start | bytes 49156
  2.3 18.8 %copy-start.1 = (f32[256,256]{1,0:T(8,128)S(1)}, f32[256,256]{1,0:T(8,128)}, u32[]{:S(2)}) copy-start(f32[256,256]{1,0:T(8,128)} %constant.4.clone.table_ref) | copy-start | bytes 786436
  2.4 3.4 %collective-permute-start = (f32[20,2,8,128]{3,2,1,0:T(8,128)S(1)}, f32[20,2,8,128]{3,2,1,0:T(8,128)S(1)}, u32[]{:S(2)}, u32[]{:S(2)}) collective-permute-start(f32[20,2,8,128]{3,2,1,0:T(8,128)S(1)} %edge.1), channel_id=1, source_target_pairs={{0,1},{1,0},{2,3},{3,2},{4,5},{5,4},{6,7},{7,6},{8,9},{9,8},{10,11... | collective-permute-start | bytes 491528 | tf_op jit(solution)/shard_map/ppermute | solution.py:254
  5.9 14.0 %collective-permute-start.1 = (f32[20,24,128]{2,1,0:T(8,128)S(1)}, f32[20,24,128]{2,1,0:T(8,128)S(1)}, u32[]{:S(2)}, u32[]{:S(2)}) collective-permute-start(f32[20,24,128]{2,1,0:T(8,128)S(1)} %get-tuple-element.6.up_ref), channel_id=1, source_target_pairs={{0,2},{2,4},{4,6},{6,8},{8,10},{10,12},{12,14},{14,16},{16,18},{18... | collective-permute-start | bytes 737288 | tf_op jit(solution)/shard_map/ppermute | solution.py:257
  9.3 11.8 %collective-permute-start.2 = (f32[20,24,128]{2,1,0:T(8,128)S(1)}, f32[20,24,128]{2,1,0:T(8,128)S(1)}, u32[]{:S(2)}, u32[]{:S(2)}) collective-permute-start(f32[20,24,128]{2,1,0:T(8,128)S(1)} %get-tuple-element.7.down_ref), channel_id=1, source_target_pairs={{2,0},{4,2},{6,4},{8,6},{10,8},{12,10},{14,12},{16,14},{18,16},{20... | collective-permute-start | bytes 737288 | tf_op jit(solution)/shard_map/ppermute | solution.py:258
  22.4 42.2 %copy-start.2 = (f32[128,256]{1,0:T(8,128)S(1)}, f32[128,256]{1,0:T(8,128)}, u32[]{:S(2)}) copy-start(f32[128,256]{1,0:T(8,128)} %constant.5.clone.table_ref) | copy-start | bytes 393220

commit v2 on v1

--- a/solution.py
+++ b/solution.py
@@ -83,7 +83,15 @@
     return out
 
 
-def edge_kernel(pops_ref, flags_ref, edge_ref):
+def edge_kernel(pops_hbm, flags_hbm, edge_ref, pops_ref, flags_ref, sems):
+    copies = [
+        pltpu.make_async_copy(pops_hbm, pops_ref, sems.at[0]),
+        pltpu.make_async_copy(flags_hbm, flags_ref, sems.at[1]),
+    ]
+    for copy in copies:
+        copy.start()
+    for copy in copies:
+        copy.wait()
     lower = lax.broadcasted_iota(jnp.int32, (8, 128), 0) < HALO
     for plane in range(2):
         for i in range(len(DIRS)):
@@ -92,7 +100,7 @@
         edge_ref[len(DIRS), plane] = flags.astype(jnp.float32)
 
 
-def first_kernel(pops_ref, flags_ref, edge_ref, up_ref, down_ref):
+def first_kernel(odd_ref, pops_ref, flags_ref, edge_ref, up_ref, down_ref, inner_ref, outer_ref):
     for plane in range(2):
         for tile in range(3):
             rows = slice(8 * tile, 8 * tile + 8)
@@ -113,6 +121,11 @@
             for i in far_dirs:
                 far_ref[far_slot[i], rows] = out[i]
             near[FLAG, rows] = flags
+    odd = jnp.full(up_ref.shape[1:], odd_ref[0]) == 1
+    for slot in range(UNITS):
+        up, down = up_ref[slot], down_ref[slot]
+        inner_ref[slot] = jnp.where(odd, down, up)
+        outer_ref[slot] = jnp.where(odd, up, down)
 
 
 def shifted(value, direction):
@@ -124,7 +137,16 @@
     return value
 
 
-def second_kernel(up_ref, down_ref, below_ref, above_ref, table_ref, final_ref, send_ref, passed_ref, relaxed_ref, spread_ref):
+def second_kernel(
+    odd_ref, up_ref, down_ref, inner_ref, outer_ref, table_ref,
+    final_ref, send_ref,
+    below_ref, above_ref, passed_ref, relaxed_ref, spread_ref,
+):
+    odd = jnp.full(up_ref.shape[1:], odd_ref[0]) == 1
+    for slot in range(UNITS):
+        inner, outer = inner_ref[slot], outer_ref[slot]
+        below_ref[slot] = jnp.where(odd, inner, outer)
+        above_ref[slot] = jnp.where(odd, outer, inner)
     near = ((below_ref, UP_SLOT), (down_ref, DOWN_SLOT), (up_ref, UP_SLOT), (above_ref, DOWN_SLOT))
     from_below = ((below_ref, UP_FAR), (below_ref, UP_SLOT), (up_ref, UP_FAR), (up_ref, UP_SLOT))
     from_above = ((down_ref, DOWN_SLOT), (down_ref, DOWN_FAR), (above_ref, DOWN_SLOT), (above_ref, DOWN_FAR))
@@ -228,7 +250,7 @@
     return table
 
 
-def call(kernel, outs, scratch=(), name=None):
+def call(kernel, outs, scratch=(), spaces=None):
     vmem = pl.BlockSpec(memory_space=pltpu.VMEM)
 
     def run(*operands):
@@ -236,11 +258,10 @@
         return pl.pallas_call(
             kernel,
             out_shape=shapes,
-            in_specs=[vmem] * len(operands),
+            in_specs=[pl.BlockSpec(memory_space=space) for space in spaces] if spaces else [vmem] * len(operands),
             out_specs=[vmem] * len(outs),
-            scratch_shapes=[pltpu.VMEM(shape, jnp.float32) for shape in scratch],
+            scratch_shapes=[pltpu.VMEM(part, jnp.float32) if isinstance(part, tuple) else part for part in scratch],
             compiler_params=pltpu.CompilerParams(vmem_limit_bytes=VMEM_BYTES),
-            name=name,
         )(*operands)
 
     return run
@@ -250,21 +271,33 @@
     slabs = lax.axis_size("slab")
     dirs, planes, rows, nodes = populations.shape
     held = rows + 2 * HALO
-    (edge,) = call(edge_kernel, [(dirs + 1, planes, 8, nodes)], name="edge")(populations, wall_flags)
+    (edge,) = call(
+        edge_kernel,
+        [(dirs + 1, planes, 8, nodes)],
+        scratch=[
+            populations.shape,
+            pltpu.VMEM(wall_flags.shape, jnp.int32),
+            pltpu.SemaphoreType.DMA((2,)),
+        ],
+        spaces=[pltpu.HBM] * 2,
+    )(*(pltpu.with_memory_space_constraint(part, pltpu.HBM) for part in (populations, wall_flags)))
     edge = lax.ppermute(edge, "col", [(0, 1), (1, 0)])
+    odd = (lax.axis_index("slab") % 2).astype(jnp.int32).reshape(1)
     message = (UNITS, held, nodes)
-    up, down = call(first_kernel, [message, message], name="first")(populations, wall_flags, edge)
-    below = lax.ppermute(up, "slab", [(i, (i + 1) % slabs) for i in range(slabs)])
-    above = lax.ppermute(down, "slab", [((i + 1) % slabs, i) for i in range(slabs)])
+    up, down, inner, outer = call(
+        first_kernel, [message] * 4, spaces=[pltpu.SMEM] + [pltpu.VMEM] * 3
+    )(odd, populations, wall_flags, edge)
+    outer = lax.ppermute(outer, "slab", [(i, (i + (1 if i % 2 else -1)) % slabs) for i in range(slabs)])
+    inner = lax.ppermute(inner, "slab", [(i, i ^ 1) for i in range(slabs)])
     final, send = call(
         second_kernel,
         [populations.shape, (slabs, 128)],
-        scratch=[(4, dirs, held, nodes), (4, dirs, held, nodes), (128, 256)],
-        name="second",
-    )(up, down, below, above, jnp.asarray(x_table(nodes)))
+        scratch=[message, message, (4, dirs, held, nodes), (4, dirs, held, nodes), (128, 256)],
+        spaces=[pltpu.SMEM] + [pltpu.VMEM] * 5,
+    )(odd, up, down, inner, outer, jnp.asarray(x_table(nodes)))
     got = lax.all_to_all(send, "slab", 0, 0, tiled=True)
     (image,) = call(
-        functools.partial(render_kernel, planes * slabs), [(4, 2, 4 * rows)], name="render"
+        functools.partial(render_kernel, planes * slabs), [(4, 2, 4 * rows)]
     )(got, jnp.asarray(y_table(rows)))
     return jnp.transpose(image, (0, 2, 1)), final
 

time: 66.1 us -> 64.8 us (0.980)
  blocking collectives: 42.1 us -> 39.4 us
  waiting for transfers between devices: 6.86 us -> 9.02 us
  local copies, waits for them, and re-layouts: 1.69 us -> 0.02 us
  Pallas kernels: 2.64 us -> 3.72 us
    all_to_all x1, blocking collectives: 42.1 us -> 39.4 us  [body(): got = lax.all_to_all(send, 'slab', 0, 0, tiled=True)]
    ppermute x2, waiting for transfers between devices: 5.5 us -> 7.69 us  [the longest x1 4.32 us: body(): inner = lax.ppermute(inner, 'slab', [(i, i ^ 1) for i in range(slabs)])]
    unnamed x8, local copies, waits for them, and re-layouts: 1.69 us -> 0.02 us
    pallas_call x4, Pallas kernels: 2.64 us -> 3.72 us  [run(): pl.pallas_call(kernel, out_shape=shapes, in_specs=[pl.BlockSpec(memory_sp...]
where the time goes in v2:
time: 64.8 us; the launch traced here: 64.5 us
  blocking collectives  39.4 us (61%)
  starting transfers between devices  11.6 us (18%)
  waiting for transfers between devices  9.02 us (14%)
  Pallas kernels  3.72 us (6%)
  between operations  0.71 us (1%)
    all_to_all x1, blocking collectives, body(): got = lax.all_to_all(send, 'slab', 0, 0, tiled=True)  39.4 us
    ppermute x1, starting transfers between devices, body(): inner = lax.ppermute(inner, 'slab', [(i, i ^ 1) for i in range(slabs)])  7.79 us
    ppermute x1, waiting for transfers between devices, body(): inner = lax.ppermute(inner, 'slab', [(i, i ^ 1) for i in range(slabs)])  4.32 us
    pallas_call x4, Pallas kernels, run(): pl.pallas_call(kernel, out_shape=shapes, in_specs=[pl.BlockSpec(memory_sp...  3.72 us
    ppermute x1, waiting for transfers between devices, body(): lax.ppermute(outer, 'slab', [(i, (i + (1 if i % 2 else -1)) % slabs) for...  3.37 us
    ppermute x1, starting transfers between devices, body(): edge = lax.ppermute(edge, 'col', [(0, 1), (1, 0)])  1.92 us
    ppermute x1, starting transfers between devices, body(): lax.ppermute(outer, 'slab', [(i, (i + (1 if i % 2 else -1)) % slabs) for...  1.92 us
    ppermute x1, waiting for transfers between devices, body(): edge = lax.ppermute(edge, 'col', [(0, 1), (1, 0)])  1.34 us
  transfers between devices with their start and end apart: 3, of which 3 were waited for; matrix products, arithmetic and copies ran while one was open for 0% of the time, Pallas kernels for 0%

profile of v2, /device:TPU:2, one launch (start us, length us, event | category | flops | bytes accessed | tf_op | source)
XLA Modules:
  0.0 64.5 jit_solution(3893094745402785402)
XLA Ops:
  0.6 0.0 copy-start
  0.6 1.1 %shard_map.59 = f32[20,2,8,128]{3,2,1,0:T(8,128)S(1)} custom-call(f32[19,2,16,128]{3,2,1,0:T(8,128)} %pops_ref.1, s32[2,16,128]{2,1,0:T(8,128)} %flags_ref.1), custom_call_target="tpu_custom_call" | custom-call | tf_op jit(solution)/shard_map/pallas_call | solution.py:258
  1.7 0.0 copy-start.3
  1.7 1.9 %collective-permute-start = (f32[20,2,8,128]{3,2,1,0:T(8,128)S(1)}, f32[20,2,8,128]{3,2,1,0:T(8,128)S(1)}, u32[]{:S(2)}, u32[]{:S(2)}) collective-permute-start(f32[20,2,8,128]{3,2,1,0:T(8,128)S(1)} %shard_map.59), channel_id=1, source_target_pairs={{0,1},{1,0},{2,3},{3,2},{4,5},{5,4},{6,7},{7,6},{8,9},{9,8},{10,11... | collective-permute-start | bytes 491528 | tf_op jit(solution)/shard_map/ppermute | solution.py:284
  3.7 0.0 copy-start.1
  3.7 1.3 %collective-permute-done.edge_ref = f32[20,2,8,128]{3,2,1,0:T(8,128)S(1)} collective-permute-done((f32[20,2,8,128]{3,2,1,0:T(8,128)S(1)}, f32[20,2,8,128]{3,2,1,0:T(8,128)S(1)}, u32[]{:S(2)}, u32[]{:S(2)}) %collective-permute-start) | collective-permute-done | bytes 163872 | tf_op jit(solution)/shard_map/ppermute | solution.py:284
  5.0 0.0 copy-done
  5.0 0.0 copy-done.3
  5.0 0.2 shard_map.60
  5.2 7.8 %collective-permute-start.1 = (f32[20,24,128]{2,1,0:T(8,128)S(1)}, f32[20,24,128]{2,1,0:T(8,128)S(1)}, u32[]{:S(2)}, u32[]{:S(2)}) collective-permute-start(f32[20,24,128]{2,1,0:T(8,128)S(1)} %get-tuple-element.10), channel_id=1, source_target_pairs={{0,2},{2,0},{4,6},{6,4},{8,10},{10,8},{12,14},{14,12},{16,18},{18,... | collective-permute-start | bytes 737288 | tf_op jit(solution)/shard_map/ppermute | solution.py:291
  13.0 1.9 %collective-permute-start.2 = (f32[20,24,128]{2,1,0:T(8,128)S(1)}, f32[20,24,128]{2,1,0:T(8,128)S(1)}, u32[]{:S(2)}, u32[]{:S(2)}) collective-permute-start(f32[20,24,128]{2,1,0:T(8,128)S(1)} %get-tuple-element.11), channel_id=1, source_target_pairs={{0,510},{2,4},{4,2},{6,8},{8,6},{10,12},{12,10},{14,16},{16,14},{1... | collective-permute-start | bytes 737288 | tf_op jit(solution)/shard_map/ppermute | solution.py:290
  14.9 4.3 %collective-permute-done.1.inner_ref = f32[20,24,128]{2,1,0:T(8,128)S(1)} collective-permute-done((f32[20,24,128]{2,1,0:T(8,128)S(1)}, f32[20,24,128]{2,1,0:T(8,128)S(1)}, u32[]{:S(2)}, u32[]{:S(2)}) %collective-permute-start.1) | collective-permute-done | bytes 245792 | tf_op jit(solution)/shard_map/ppermute | solution.py:291
  19.2 3.4 %collective-permute-done.2.outer_ref = f32[20,24,128]{2,1,0:T(8,128)S(1)} collective-permute-done((f32[20,24,128]{2,1,0:T(8,128)S(1)}, f32[20,24,128]{2,1,0:T(8,128)S(1)}, u32[]{:S(2)}, u32[]{:S(2)}) %collective-permute-start.2) | collective-permute-done | bytes 245792 | tf_op jit(solution)/shard_map/ppermute | solution.py:290
  22.6 0.0 copy-done.1
  22.6 1.2 %shard_map.61 = (f32[19,2,16,128]{3,2,1,0:T(8,128)}, f32[256,128]{1,0:T(8,128)S(1)}) custom-call(s32[1]{0:T(128)} %bitcast.odd_ref, f32[20,24,128]{2,1,0:T(8,128)S(1)} %get-tuple-element.8.up_ref, f32[20,24,128]{2,1,0:T(8,128)S(1)} %get-tuple-element.9.down_ref, f32[20,24,128]{2,1,0:T(8,128)S(1)} %collective-permute-done.1.inner_ref, ...), custom_call_target="tpu_custom_call" | custom-call | tf_op jit(solution)/shard_map/pallas_call | solution.py:258
  23.8 0.0 copy-start.2
  23.9 39.4 %all_to_all.11 = f32[256,1,128]{2,1,0:T(1,128)S(1)} all-to-all(f32[256,1,128]{2,1,0:T(1,128)S(1)} %bitcast.7), channel_id=1, replica_groups=mesh['slab'=256,'col'=2] {'slab'}, dimensions={0} | all-to-all | bytes 262144 | tf_op jit(solution)/shard_map/all_to_all | solution.py:298
  63.3 0.0 copy-done.2
  63.3 1.2 %shard_map.62 = f32[4,2,64]{2,1,0:T(2,128)} custom-call(f32[256,128]{1,0:T(8,128)S(1)} %bitcast.6, f32[128,256]{1,0:T(8,128)S(1)} %copy-done.2), custom_call_target="tpu_custom_call" | custom-call | tf_op jit(solution)/shard_map/pallas_call | solution.py:258
Async XLA Ops:
  0.6 4.4 %copy-start = (f32[19,2,16,128]{3,2,1,0:T(8,128)S(1)}, f32[19,2,16,128]{3,2,1,0:T(8,128)}, u32[]{:S(2)}) copy-start(f32[19,2,16,128]{3,2,1,0:T(8,128)} %pops_ref.1) | copy-start | bytes 933892
  1.7 3.3 %copy-start.3 = (s32[2,16,128]{2,1,0:T(8,128)S(1)}, s32[2,16,128]{2,1,0:T(8,128)}, u32[]{:S(2)}) copy-start(s32[2,16,128]{2,1,0:T(8,128)} %flags_ref.1) | copy-start | bytes 49156
  1.7 3.3 %collective-permute-start = (f32[20,2,8,128]{3,2,1,0:T(8,128)S(1)}, f32[20,2,8,128]{3,2,1,0:T(8,128)S(1)}, u32[]{:S(2)}, u32[]{:S(2)}) collective-permute-start(f32[20,2,8,128]{3,2,1,0:T(8,128)S(1)} %shard_map.59), channel_id=1, source_target_pairs={{0,1},{1,0},{2,3},{3,2},{4,5},{5,4},{6,7},{7,6},{8,9},{9,8},{10,11... | collective-permute-start | bytes 491528 | tf_op jit(solution)/shard_map/ppermute | solution.py:284
  3.7 19.0 %copy-start.1 = (f32[256,256]{1,0:T(8,128)S(1)}, f32[256,256]{1,0:T(8,128)}, u32[]{:S(2)}) copy-start(f32[256,256]{1,0:T(8,128)} %constant.23.clone.table_ref) | copy-start | bytes 786436
  5.2 14.0 %collective-permute-start.1 = (f32[20,24,128]{2,1,0:T(8,128)S(1)}, f32[20,24,128]{2,1,0:T(8,128)S(1)}, u32[]{:S(2)}, u32[]{:S(2)}) collective-permute-start(f32[20,24,128]{2,1,0:T(8,128)S(1)} %get-tuple-element.10), channel_id=1, source_target_pairs={{0,2},{2,0},{4,6},{6,4},{8,10},{10,8},{12,14},{14,12},{16,18},{18,... | collective-permute-start | bytes 737288 | tf_op jit(solution)/shard_map/ppermute | solution.py:291
  13.0 9.6 %collective-permute-start.2 = (f32[20,24,128]{2,1,0:T(8,128)S(1)}, f32[20,24,128]{2,1,0:T(8,128)S(1)}, u32[]{:S(2)}, u32[]{:S(2)}) collective-permute-start(f32[20,24,128]{2,1,0:T(8,128)S(1)} %get-tuple-element.11), channel_id=1, source_target_pairs={{0,510},{2,4},{4,2},{6,8},{8,6},{10,12},{12,10},{14,16},{16,14},{1... | collective-permute-start | bytes 737288 | tf_op jit(solution)/shard_map/ppermute | solution.py:290
  23.8 39.4 %copy-start.2 = (f32[128,256]{1,0:T(8,128)S(1)}, f32[128,256]{1,0:T(8,128)}, u32[]{:S(2)}) copy-start(f32[128,256]{1,0:T(8,128)} %constant.24.clone.table_ref) | copy-start | bytes 393220

commit v3 on v2

--- a/solution.py
+++ b/solution.py
@@ -23,12 +23,11 @@
 SPEED_GAIN = 10000.0
 OPTICAL = 2.0
 
-FLAG = len(MID) + 2 * len(UP)
+MOMENTS = len(UP)
+FLAG = MOMENTS + 4
 UNITS = FLAG + 1
-UP_SLOT = {d: k for k, d in enumerate(MID + UP)}
-UP_FAR = {d: len(MID) + len(UP) + k for k, d in enumerate(UP)}
-DOWN_SLOT = {d: k for k, d in enumerate(MID + DOWN)}
-DOWN_FAR = {d: len(MID) + len(DOWN) + k for k, d in enumerate(DOWN)}
+UP_SLOT = {d: k for k, d in enumerate(UP)}
+DOWN_SLOT = {d: k for k, d in enumerate(DOWN)}
 
 VMEM_BYTES = 12 << 20
 HALO = 4
@@ -43,28 +42,26 @@
     return total
 
 
-def add_moments(state):
-    density = state[0]
-    momentum = [None, None, None]
-    for i in range(1, len(DIRS)):
-        density = density + state[i]
-        for axis, element in enumerate(DIRS[i]):
+def add_moments(total, state):
+    total = list(total) if total else [None] * 4
+    for i, value in state.items():
+        for part, element in enumerate((1,) + DIRS[i]):
             if element:
-                held = momentum[axis]
+                held = total[part]
                 if held is None:
-                    momentum[axis] = state[i] if element > 0 else -state[i]
+                    total[part] = value if element > 0 else -value
                 else:
-                    momentum[axis] = held + state[i] if element > 0 else held - state[i]
-    return density, momentum
-
-
-def relax(state, wall, wanted):
-    density, momentum = add_moments(state)
+                    total[part] = held + value if element > 0 else held - value
+    return total
+
+
+def relax(total, state, wall, wanted):
+    density = total[0]
     inverse = 1.0 / density
-    velocity = [part * inverse for part in momentum]
+    velocity = [part * inverse for part in total[1:]]
     speed_sq = velocity[0] * velocity[0] + velocity[1] * velocity[1] + velocity[2] * velocity[2]
     rest = 1.0 - 1.5 * speed_sq
-    scaled = {w: w * density for w in set(WEIGHTS)}
+    scaled = {w: w * density for w in sorted(set(WEIGHTS))}
     out = {}
     for i, direction in enumerate(DIRS):
         if i > OPP[i] or (i not in wanted and OPP[i] not in wanted):
@@ -100,27 +97,34 @@
         edge_ref[len(DIRS), plane] = flags.astype(jnp.float32)
 
 
-def first_kernel(odd_ref, pops_ref, flags_ref, edge_ref, up_ref, down_ref, inner_ref, outer_ref):
-    for plane in range(2):
+def first_kernel(
+    odd_ref, pops_ref, flags_ref, edge_ref,
+    passed_ref, up_ref, down_ref, inner_ref, outer_ref,
+    relaxed_ref,
+):
+    for plane, near in ((0, down_ref), (1, up_ref)):
         for tile in range(3):
             rows = slice(8 * tile, 8 * tile + 8)
             if tile < 2:
-                state = [pops_ref[i, plane, rows] for i in range(len(DIRS))]
+                state = {i: pops_ref[i, plane, rows] for i in range(len(DIRS))}
                 flags = flags_ref[plane, rows].astype(jnp.float32)
             else:
-                state = [edge_ref[i, plane] for i in range(len(DIRS))]
+                state = {i: edge_ref[i, plane] for i in range(len(DIRS))}
                 flags = edge_ref[len(DIRS), plane]
-            out = relax(state, flags > 0.5, range(len(DIRS)))
-            near, far_slot, near_slot, far_ref, far_dirs = (
-                (down_ref, UP_FAR, DOWN_SLOT, up_ref, UP)
-                if plane == 0
-                else (up_ref, DOWN_FAR, UP_SLOT, down_ref, DOWN)
-            )
-            for i, slot in near_slot.items():
-                near[slot, rows] = out[i]
-            for i in far_dirs:
-                far_ref[far_slot[i], rows] = out[i]
+            out = relax(add_moments(None, state), state, flags > 0.5, range(len(DIRS)))
+            for i, value in out.items():
+                relaxed_ref[plane, i, rows] = value
             near[FLAG, rows] = flags
+    for plane, near, slots, inward in ((0, down_ref, DOWN_SLOT, DOWN), (1, up_ref, UP_SLOT, UP)):
+        total = None
+        for i in MID + inward:
+            value = shifted(relaxed_ref[plane if i in MID else 1 - plane, i], DIRS[i])
+            passed_ref[plane, i] = value
+            total = add_moments(total, {i: value})
+        for part, value in enumerate(total):
+            near[MOMENTS + part] = value
+        for i, slot in slots.items():
+            near[slot] = shifted(relaxed_ref[plane, i], DIRS[i])
     odd = jnp.full(up_ref.shape[1:], odd_ref[0]) == 1
     for slot in range(UNITS):
         up, down = up_ref[slot], down_ref[slot]
@@ -138,39 +142,40 @@
 
 
 def second_kernel(
-    odd_ref, up_ref, down_ref, inner_ref, outer_ref, table_ref,
+    odd_ref, passed_ref, up_ref, down_ref, inner_ref, outer_ref, table_ref,
     final_ref, send_ref,
-    below_ref, above_ref, passed_ref, relaxed_ref, spread_ref,
+    below_ref, above_ref, relaxed_ref, spread_ref,
 ):
     odd = jnp.full(up_ref.shape[1:], odd_ref[0]) == 1
     for slot in range(UNITS):
         inner, outer = inner_ref[slot], outer_ref[slot]
         below_ref[slot] = jnp.where(odd, inner, outer)
         above_ref[slot] = jnp.where(odd, outer, inner)
-    near = ((below_ref, UP_SLOT), (down_ref, DOWN_SLOT), (up_ref, UP_SLOT), (above_ref, DOWN_SLOT))
-    from_below = ((below_ref, UP_FAR), (below_ref, UP_SLOT), (up_ref, UP_FAR), (up_ref, UP_SLOT))
-    from_above = ((down_ref, DOWN_SLOT), (down_ref, DOWN_FAR), (above_ref, DOWN_SLOT), (above_ref, DOWN_FAR))
-    wanted = (UP, range(len(DIRS)), range(len(DIRS)), DOWN)
     spread_ref[...] = jnp.zeros(spread_ref.shape, jnp.float32)
-    for plane in range(4):
-        for i, direction in enumerate(DIRS):
-            ref, slots = (near, from_below, from_above)[direction[2]][plane]
-            passed_ref[plane, i] = shifted(ref[slots[i]], direction)
+    sides = (
+        (below_ref, down_ref, DOWN_SLOT, UP),
+        (down_ref, below_ref, UP_SLOT, range(len(DIRS))),
+        (up_ref, above_ref, DOWN_SLOT, range(len(DIRS))),
+        (above_ref, up_ref, UP_SLOT, DOWN),
+    )
+    for plane, (near, other, slots, wanted) in enumerate(sides):
         for tile in range(3):
             rows = slice(8 * tile, 8 * tile + 8)
-            state = [passed_ref[plane, i, rows] for i in range(len(DIRS))]
-            out = relax(state, near[plane][0][FLAG, rows] > 0.5, wanted[plane])
-            for i in wanted[plane]:
+            state = {i: other[slot, rows] for i, slot in slots.items()}
+            total = add_moments([near[MOMENTS + part, rows] for part in range(4)], state)
+            if plane in (1, 2):
+                state.update({i: passed_ref[plane - 1, i, rows] for i in range(len(DIRS)) if i not in slots})
+            out = relax(total, state, near[FLAG, rows] > 0.5, wanted)
+            for i in wanted:
                 relaxed_ref[plane, i, rows] = out[i]
     for plane in range(2):
-        state = []
+        total = None
         for i, direction in enumerate(DIRS):
             value = shifted(relaxed_ref[plane + 1 - direction[2], i], direction)
             final_ref[i, plane] = value[0:16]
-            state.append(value)
-        density, momentum = add_moments(state)
-        inverse = 1.0 / density
-        velocity = [part * inverse for part in momentum]
+            total = add_moments(total, {i: value})
+        inverse = 1.0 / total[0]
+        velocity = [part * inverse for part in total[1:]]
         scalar = SPEED_GAIN * (velocity[0] * velocity[0] + velocity[1] * velocity[1] + velocity[2] * velocity[2])
         spread_ref[24 * plane : 24 * plane + 24, 0:128] = scalar
         spread_ref[64 + 24 * plane : 64 + 24 * plane + 24, 128:256] = scalar
@@ -284,17 +289,18 @@
     edge = lax.ppermute(edge, "col", [(0, 1), (1, 0)])
     odd = (lax.axis_index("slab") % 2).astype(jnp.int32).reshape(1)
     message = (UNITS, held, nodes)
-    up, down, inner, outer = call(
-        first_kernel, [message] * 4, spaces=[pltpu.SMEM] + [pltpu.VMEM] * 3
+    lattice = (2, dirs, held, nodes)
+    passed, up, down, inner, outer = call(
+        first_kernel, [lattice] + [message] * 4, scratch=[lattice], spaces=[pltpu.SMEM] + [pltpu.VMEM] * 3
     )(odd, populations, wall_flags, edge)
     outer = lax.ppermute(outer, "slab", [(i, (i + (1 if i % 2 else -1)) % slabs) for i in range(slabs)])
     inner = lax.ppermute(inner, "slab", [(i, i ^ 1) for i in range(slabs)])
     final, send = call(
         second_kernel,
         [populations.shape, (slabs, 128)],
-        scratch=[message, message, (4, dirs, held, nodes), (4, dirs, held, nodes), (128, 256)],
-        spaces=[pltpu.SMEM] + [pltpu.VMEM] * 5,
-    )(odd, up, down, inner, outer, jnp.asarray(x_table(nodes)))
+        scratch=[message, message, (4, dirs, held, nodes), (128, 256)],
+        spaces=[pltpu.SMEM] + [pltpu.VMEM] * 6,
+    )(odd, passed, up, down, inner, outer, jnp.asarray(x_table(nodes)))
     got = lax.all_to_all(send, "slab", 0, 0, tiled=True)
     (image,) = call(
         functools.partial(render_kernel, planes * slabs), [(4, 2, 4 * rows)]

time: 64.8 us -> 62.1 us (0.958)
  waiting for transfers between devices: 9.02 us -> 6.39 us
    ppermute x1, waiting for transfers between devices: 4.32 us -> 1.69 us  [body(): inner = lax.ppermute(inner, 'slab', [(i, i ^ 1) for i in range(slabs)])]
where the time goes in v3:
time: 62.1 us; the launch traced here: 61.8 us
  blocking collectives  39.4 us (63%)
  starting transfers between devices  11.6 us (19%)
  waiting for transfers between devices  6.39 us (10%)
  Pallas kernels  3.62 us (6%)
  between operations  0.71 us (1%)
    all_to_all x1, blocking collectives, body(): got = lax.all_to_all(send, 'slab', 0, 0, tiled=True)  39.4 us
    ppermute x1, starting transfers between devices, body(): inner = lax.ppermute(inner, 'slab', [(i, i ^ 1) for i in range(slabs)])  7.79 us
    pallas_call x4, Pallas kernels, run(): pl.pallas_call(kernel, out_shape=shapes, in_specs=[pl.BlockSpec(memory_sp...  3.62 us
    ppermute x1, waiting for transfers between devices, body(): lax.ppermute(outer, 'slab', [(i, (i + (1 if i % 2 else -1)) % slabs) for...  3.37 us
    ppermute x1, starting transfers between devices, body(): edge = lax.ppermute(edge, 'col', [(0, 1), (1, 0)])  1.92 us
    ppermute x1, starting transfers between devices, body(): lax.ppermute(outer, 'slab', [(i, (i + (1 if i % 2 else -1)) % slabs) for...  1.92 us
    ppermute x1, waiting for transfers between devices, body(): inner = lax.ppermute(inner, 'slab', [(i, i ^ 1) for i in range(slabs)])  1.69 us
    ppermute x1, waiting for transfers between devices, body(): edge = lax.ppermute(edge, 'col', [(0, 1), (1, 0)])  1.34 us
  transfers between devices with their start and end apart: 3, of which 3 were waited for; matrix products, arithmetic and copies ran while one was open for 0% of the time, Pallas kernels for 0%

profile of v3, /device:TPU:2, one launch (start us, length us, event | category | flops | bytes accessed | tf_op | source)
XLA Modules:
  0.0 61.8 jit_solution(14874581820120841200)
XLA Ops:
  0.6 0.0 copy-start
  0.6 1.1 %shard_map.59 = f32[20,2,8,128]{3,2,1,0:T(8,128)S(1)} custom-call(f32[19,2,16,128]{3,2,1,0:T(8,128)} %pops_ref.1, s32[2,16,128]{2,1,0:T(8,128)} %flags_ref.1), custom_call_target="tpu_custom_call" | custom-call | tf_op jit(solution)/shard_map/pallas_call | solution.py:263
  1.7 0.0 copy-start.3
  1.7 1.9 %collective-permute-start = (f32[20,2,8,128]{3,2,1,0:T(8,128)S(1)}, f32[20,2,8,128]{3,2,1,0:T(8,128)S(1)}, u32[]{:S(2)}, u32[]{:S(2)}) collective-permute-start(f32[20,2,8,128]{3,2,1,0:T(8,128)S(1)} %shard_map.59), channel_id=1, source_target_pairs={{0,1},{1,0},{2,3},{3,2},{4,5},{5,4},{6,7},{7,6},{8,9},{9,8},{10,11... | collective-permute-start | bytes 491528 | tf_op jit(solution)/shard_map/ppermute | solution.py:289
  3.7 0.0 copy-start.1
  3.7 1.3 %collective-permute-done.edge_ref = f32[20,2,8,128]{3,2,1,0:T(8,128)S(1)} collective-permute-done((f32[20,2,8,128]{3,2,1,0:T(8,128)S(1)}, f32[20,2,8,128]{3,2,1,0:T(8,128)S(1)}, u32[]{:S(2)}, u32[]{:S(2)}) %collective-permute-start) | collective-permute-done | bytes 163872 | tf_op jit(solution)/shard_map/ppermute | solution.py:289
  5.0 0.0 copy-done
  5.0 0.0 copy-done.3
  5.0 0.2 shard_map.60
  5.3 7.8 %collective-permute-start.1 = (f32[10,24,128]{2,1,0:T(8,128)S(1)}, f32[10,24,128]{2,1,0:T(8,128)S(1)}, u32[]{:S(2)}, u32[]{:S(2)}) collective-permute-start(f32[10,24,128]{2,1,0:T(8,128)S(1)} %get-tuple-element.12), channel_id=1, source_target_pairs={{0,2},{2,0},{4,6},{6,4},{8,10},{10,8},{12,14},{14,12},{16,18},{18,... | collective-permute-start | bytes 368648 | tf_op jit(solution)/shard_map/ppermute | solution.py:297
  13.1 1.9 %collective-permute-start.2 = (f32[10,24,128]{2,1,0:T(8,128)S(1)}, f32[10,24,128]{2,1,0:T(8,128)S(1)}, u32[]{:S(2)}, u32[]{:S(2)}) collective-permute-start(f32[10,24,128]{2,1,0:T(8,128)S(1)} %get-tuple-element.13), channel_id=1, source_target_pairs={{0,510},{2,4},{4,2},{6,8},{8,6},{10,12},{12,10},{14,16},{16,14},{1... | collective-permute-start | bytes 368648 | tf_op jit(solution)/shard_map/ppermute | solution.py:296
  15.0 1.7 %collective-permute-done.1.inner_ref = f32[10,24,128]{2,1,0:T(8,128)S(1)} collective-permute-done((f32[10,24,128]{2,1,0:T(8,128)S(1)}, f32[10,24,128]{2,1,0:T(8,128)S(1)}, u32[]{:S(2)}, u32[]{:S(2)}) %collective-permute-start.1) | collective-permute-done | bytes 122912 | tf_op jit(solution)/shard_map/ppermute | solution.py:297
  16.7 3.4 %collective-permute-done.2.outer_ref = f32[10,24,128]{2,1,0:T(8,128)S(1)} collective-permute-done((f32[10,24,128]{2,1,0:T(8,128)S(1)}, f32[10,24,128]{2,1,0:T(8,128)S(1)}, u32[]{:S(2)}, u32[]{:S(2)}) %collective-permute-start.2) | collective-permute-done | bytes 122912 | tf_op jit(solution)/shard_map/ppermute | solution.py:296
  20.0 0.0 copy-done.1
  20.0 1.1 %shard_map.61 = (f32[19,2,16,128]{3,2,1,0:T(8,128)}, f32[256,128]{1,0:T(8,128)S(1)}) custom-call(s32[1]{0:T(128)} %bitcast.odd_ref, f32[2,19,24,128]{3,2,1,0:T(8,128)S(1)} %get-tuple-element.9.passed_ref, f32[10,24,128]{2,1,0:T(8,128)S(1)} %get-tuple-element.10.up_ref, f32[10,24,128]{2,1,0:T(8,128)S(1)} %get-tuple-element.11.down_ref, ...), custom_call_target="tpu_custom_call" | custom-call | tf_op jit(solution)/shard_map/pallas_call | solution.py:263
  21.1 0.0 copy-start.2
  21.1 39.4 %all_to_all.11 = f32[256,1,128]{2,1,0:T(1,128)S(1)} all-to-all(f32[256,1,128]{2,1,0:T(1,128)S(1)} %bitcast.7), channel_id=1, replica_groups=mesh['slab'=256,'col'=2] {'slab'}, dimensions={0} | all-to-all | bytes 262144 | tf_op jit(solution)/shard_map/all_to_all | solution.py:304
  60.6 0.0 copy-done.2
  60.6 1.2 %shard_map.62 = f32[4,2,64]{2,1,0:T(2,128)} custom-call(f32[256,128]{1,0:T(8,128)S(1)} %bitcast.6, f32[128,256]{1,0:T(8,128)S(1)} %copy-done.2), custom_call_target="tpu_custom_call" | custom-call | tf_op jit(solution)/shard_map/pallas_call | solution.py:263
Async XLA Ops:
  0.6 4.4 %copy-start = (f32[19,2,16,128]{3,2,1,0:T(8,128)S(1)}, f32[19,2,16,128]{3,2,1,0:T(8,128)}, u32[]{:S(2)}) copy-start(f32[19,2,16,128]{3,2,1,0:T(8,128)} %pops_ref.1) | copy-start | bytes 933892
  1.7 3.3 %copy-start.3 = (s32[2,16,128]{2,1,0:T(8,128)S(1)}, s32[2,16,128]{2,1,0:T(8,128)}, u32[]{:S(2)}) copy-start(s32[2,16,128]{2,1,0:T(8,128)} %flags_ref.1) | copy-start | bytes 49156
  1.7 3.3 %collective-permute-start = (f32[20,2,8,128]{3,2,1,0:T(8,128)S(1)}, f32[20,2,8,128]{3,2,1,0:T(8,128)S(1)}, u32[]{:S(2)}, u32[]{:S(2)}) collective-permute-start(f32[20,2,8,128]{3,2,1,0:T(8,128)S(1)} %shard_map.59), channel_id=1, source_target_pairs={{0,1},{1,0},{2,3},{3,2},{4,5},{5,4},{6,7},{7,6},{8,9},{9,8},{10,11... | collective-permute-start | bytes 491528 | tf_op jit(solution)/shard_map/ppermute | solution.py:289
  3.7 16.4 %copy-start.1 = (f32[256,256]{1,0:T(8,128)S(1)}, f32[256,256]{1,0:T(8,128)}, u32[]{:S(2)}) copy-start(f32[256,256]{1,0:T(8,128)} %constant.23.clone.table_ref) | copy-start | bytes 786436
  5.3 11.4 %collective-permute-start.1 = (f32[10,24,128]{2,1,0:T(8,128)S(1)}, f32[10,24,128]{2,1,0:T(8,128)S(1)}, u32[]{:S(2)}, u32[]{:S(2)}) collective-permute-start(f32[10,24,128]{2,1,0:T(8,128)S(1)} %get-tuple-element.12), channel_id=1, source_target_pairs={{0,2},{2,0},{4,6},{6,4},{8,10},{10,8},{12,14},{14,12},{16,18},{18,... | collective-permute-start | bytes 368648 | tf_op jit(solution)/shard_map/ppermute | solution.py:297
  13.1 7.0 %collective-permute-start.2 = (f32[10,24,128]{2,1,0:T(8,128)S(1)}, f32[10,24,128]{2,1,0:T(8,128)S(1)}, u32[]{:S(2)}, u32[]{:S(2)}) collective-permute-start(f32[10,24,128]{2,1,0:T(8,128)S(1)} %get-tuple-element.13), channel_id=1, source_target_pairs={{0,510},{2,4},{4,2},{6,8},{8,6},{10,12},{12,10},{14,16},{16,14},{1... | collective-permute-start | bytes 368648 | tf_op jit(solution)/shard_map/ppermute | solution.py:296
  21.1 39.4 %copy-start.2 = (f32[128,256]{1,0:T(8,128)S(1)}, f32[128,256]{1,0:T(8,128)}, u32[]{:S(2)}) copy-start(f32[128,256]{1,0:T(8,128)} %constant.24.clone.table_ref) | copy-start | bytes 393220

commit v4 on v3

--- a/solution.py
+++ b/solution.py
@@ -30,6 +30,7 @@
 DOWN_SLOT = {d: k for k, d in enumerate(DOWN)}
 
 VMEM_BYTES = 12 << 20
+GROUP = 16
 HALO = 4
 
 
@@ -188,18 +189,16 @@
     )
 
 
-def render_kernel(total_planes, got_ref, table_ref, image_ref):
-    slabs = got_ref.shape[0]
-    groups = slabs // 8
-    ordered = jnp.concatenate([got_ref[pl.ds(j, 8, stride=groups), :] for j in range(groups)], axis=0)
+def render_kernel(total_planes, got_ref, table_ref, part_ref):
+    groups = part_ref.shape[0]
     samples = jnp.dot(
-        ordered, table_ref[...], precision=lax.Precision.HIGHEST, preferred_element_type=jnp.float32
-    )
-    depth = jnp.zeros((8, 128), jnp.float32)
-    light = [jnp.zeros((8, 128), jnp.float32) for _ in range(3)]
-    for j in range(groups):
+        got_ref[...], table_ref[...], precision=lax.Precision.HIGHEST, preferred_element_type=jnp.float32
+    )
+    depth = jnp.zeros((groups, 128), jnp.float32)
+    light = [jnp.zeros((groups, 128), jnp.float32) for _ in range(3)]
+    for source in range(got_ref.shape[0] // groups):
         for plane in range(2):
-            sample = samples[8 * j : 8 * j + 8, 128 * plane : 128 * plane + 128]
+            sample = samples[groups * source : groups * (source + 1), 128 * plane : 128 * plane + 128]
             squared = sample * sample
             green = 1.0 / (1.0 + squared)
             saturation = squared * green
@@ -213,14 +212,19 @@
             light[1] = light[1] + weight * green
             light[2] = light[2] + weight * blue
             depth = depth + extinction
-    row = lax.broadcasted_iota(jnp.int32, (8, 128), 0)
-    ahead = depth
-    for step in (1, 2, 4):
-        ahead = ahead + jnp.where(row >= step, pltpu.roll(ahead, step, 0), 0.0)
-    through = jnp.exp(depth - ahead)
-    sums = [jnp.sum(part * through, axis=0, keepdims=True) for part in light]
-    sums.append(1.0 - jnp.exp(-jnp.sum(depth, axis=0, keepdims=True)))
-    for channel, value in enumerate(sums):
+    for channel, value in enumerate(light + [depth]):
+        part_ref[:, channel, :] = value
+
+
+def compose_kernel(got_ref, image_ref):
+    ahead = jnp.zeros((1, 128), jnp.float32)
+    light = jnp.zeros((4, 128), jnp.float32)
+    for group in range(got_ref.shape[0]):
+        part = got_ref[group]
+        light = light + jnp.exp(-ahead) * part
+        ahead = ahead + part[3:4]
+    for channel in range(4):
+        value = light[channel : channel + 1] if channel < 3 else 1.0 - jnp.exp(-ahead)
         image_ref[channel, 0:1, :] = value[:, 0:64]
         image_ref[channel, 1:2, :] = value[:, 64:128]
 
@@ -235,12 +239,12 @@
     )
 
 
-def x_table(nodes):
+def x_table(nodes, group):
     table = np.zeros((2 * nodes, 2 * nodes), np.float32)
     for fine in range(4 * nodes):
         for offset, weight in zip((-1, 0, 1, 2), cubic_weights(fine - 2)):
             table[fine // 2, (fine % 2) * nodes + ((fine - 2) // 4 + offset) % nodes] += weight
-    return table
+    return table.reshape(-1, group, 2 * nodes).transpose(1, 0, 2).reshape(2 * nodes, 2 * nodes)
 
 
 def y_table(rows):
@@ -300,11 +304,14 @@
         [populations.shape, (slabs, 128)],
         scratch=[message, message, (4, dirs, held, nodes), (128, 256)],
         spaces=[pltpu.SMEM] + [pltpu.VMEM] * 6,
-    )(odd, passed, up, down, inner, outer, jnp.asarray(x_table(nodes)))
-    got = lax.all_to_all(send, "slab", 0, 0, tiled=True)
-    (image,) = call(
-        functools.partial(render_kernel, planes * slabs), [(4, 2, 4 * rows)]
-    )(got, jnp.asarray(y_table(rows)))
+    )(odd, passed, up, down, inner, outer, jnp.asarray(x_table(nodes, GROUP)))
+    count = slabs // GROUP
+    near = [[g * GROUP + i for i in range(GROUP)] for g in range(count)]
+    far = [[g * GROUP + i for g in range(count)] for i in range(GROUP)]
+    got = lax.all_to_all(send, "slab", 0, 0, axis_index_groups=near, tiled=True)
+    (part,) = call(functools.partial(render_kernel, planes * slabs), [(count, 4, 128)])(got, jnp.asarray(y_table(rows)))
+    got = lax.all_to_all(part, "slab", 0, 0, axis_index_groups=far, tiled=True)
+    (image,) = call(compose_kernel, [(4, 2, 4 * rows)])(got)
     return jnp.transpose(image, (0, 2, 1)), final
 
 

time: 62.1 us -> 63.1 us (1.016)
  blocking collectives: 39.4 us -> 40.4 us
    all_to_all x1 -> x2, blocking collectives: 39.4 us -> 40.4 us  [the longest x1 23.2 us: body(): got = lax.all_to_all(part, 'slab', 0, 0, axis_index_groups=far, tiled=True)]
    pallas_call x4 -> x5, Pallas kernels: 3.62 us -> 3.63 us  [run(): pl.pallas_call(kernel, out_shape=shapes, in_specs=[pl.BlockSpec(memory_sp...]
where the time goes in v4:
time: 63.1 us; the launch traced here: 62.8 us
  blocking collectives  40.4 us (64%)
  starting transfers between devices  11.6 us (18%)
  waiting for transfers between devices  6.39 us (10%)
  Pallas kernels  3.63 us (6%)
  between operations  0.71 us (1%)
    all_to_all x1, blocking collectives, body(): got = lax.all_to_all(part, 'slab', 0, 0, axis_index_groups=far, tiled=True)  23.2 us
    all_to_all x1, blocking collectives, body(): got = lax.all_to_all(send, 'slab', 0, 0, axis_index_groups=near, tiled=True)  17.1 us
    ppermute x1, starting transfers between devices, body(): inner = lax.ppermute(inner, 'slab', [(i, i ^ 1) for i in range(slabs)])  7.79 us
    pallas_call x5, Pallas kernels, run(): pl.pallas_call(kernel, out_shape=shapes, in_specs=[pl.BlockSpec(memory_sp...  3.63 us
    ppermute x1, waiting for transfers between devices, body(): lax.ppermute(outer, 'slab', [(i, (i + (1 if i % 2 else -1)) % slabs) for...  3.37 us
    ppermute x1, starting transfers between devices, body(): edge = lax.ppermute(edge, 'col', [(0, 1), (1, 0)])  1.92 us
    ppermute x1, starting transfers between devices, body(): lax.ppermute(outer, 'slab', [(i, (i + (1 if i % 2 else -1)) % slabs) for...  1.92 us
    ppermute x1, waiting for transfers between devices, body(): inner = lax.ppermute(inner, 'slab', [(i, i ^ 1) for i in range(slabs)])  1.69 us
  transfers between devices with their start and end apart: 3, of which 3 were waited for; matrix products, arithmetic and copies ran while one was open for 0% of the time, Pallas kernels for 0%

profile of v4, /device:TPU:2, one launch (start us, length us, event | category | flops | bytes accessed | tf_op | source)
XLA Modules:
  0.0 62.8 jit_solution(10614301591422072337)
XLA Ops:
  0.6 0.0 copy-start
  0.6 1.1 %shard_map.59 = f32[20,2,8,128]{3,2,1,0:T(8,128)S(1)} custom-call(f32[19,2,16,128]{3,2,1,0:T(8,128)} %pops_ref.1, s32[2,16,128]{2,1,0:T(8,128)} %flags_ref.1), custom_call_target="tpu_custom_call" | custom-call | tf_op jit(solution)/shard_map/pallas_call | solution.py:267
  1.7 0.0 copy-start.3
  1.7 1.9 %collective-permute-start = (f32[20,2,8,128]{3,2,1,0:T(8,128)S(1)}, f32[20,2,8,128]{3,2,1,0:T(8,128)S(1)}, u32[]{:S(2)}, u32[]{:S(2)}) collective-permute-start(f32[20,2,8,128]{3,2,1,0:T(8,128)S(1)} %shard_map.59), channel_id=1, source_target_pairs={{0,1},{1,0},{2,3},{3,2},{4,5},{5,4},{6,7},{7,6},{8,9},{9,8},{10,11... | collective-permute-start | bytes 491528 | tf_op jit(solution)/shard_map/ppermute | solution.py:293
  3.7 0.0 copy-start.1
  3.7 1.3 %collective-permute-done.edge_ref = f32[20,2,8,128]{3,2,1,0:T(8,128)S(1)} collective-permute-done((f32[20,2,8,128]{3,2,1,0:T(8,128)S(1)}, f32[20,2,8,128]{3,2,1,0:T(8,128)S(1)}, u32[]{:S(2)}, u32[]{:S(2)}) %collective-permute-start) | collective-permute-done | bytes 163872 | tf_op jit(solution)/shard_map/ppermute | solution.py:293
  5.0 0.0 copy-done
  5.0 0.0 copy-done.3
  5.0 0.2 shard_map.60
  5.3 7.8 %collective-permute-start.1 = (f32[10,24,128]{2,1,0:T(8,128)S(1)}, f32[10,24,128]{2,1,0:T(8,128)S(1)}, u32[]{:S(2)}, u32[]{:S(2)}) collective-permute-start(f32[10,24,128]{2,1,0:T(8,128)S(1)} %get-tuple-element.12), channel_id=1, source_target_pairs={{0,2},{2,0},{4,6},{6,4},{8,10},{10,8},{12,14},{14,12},{16,18},{18,... | collective-permute-start | bytes 368648 | tf_op jit(solution)/shard_map/ppermute | solution.py:301
  13.1 1.9 %collective-permute-start.2 = (f32[10,24,128]{2,1,0:T(8,128)S(1)}, f32[10,24,128]{2,1,0:T(8,128)S(1)}, u32[]{:S(2)}, u32[]{:S(2)}) collective-permute-start(f32[10,24,128]{2,1,0:T(8,128)S(1)} %get-tuple-element.13), channel_id=1, source_target_pairs={{0,510},{2,4},{4,2},{6,8},{8,6},{10,12},{12,10},{14,16},{16,14},{1... | collective-permute-start | bytes 368648 | tf_op jit(solution)/shard_map/ppermute | solution.py:300
  15.0 1.7 %collective-permute-done.1.inner_ref = f32[10,24,128]{2,1,0:T(8,128)S(1)} collective-permute-done((f32[10,24,128]{2,1,0:T(8,128)S(1)}, f32[10,24,128]{2,1,0:T(8,128)S(1)}, u32[]{:S(2)}, u32[]{:S(2)}) %collective-permute-start.1) | collective-permute-done | bytes 122912 | tf_op jit(solution)/shard_map/ppermute | solution.py:301
  16.7 3.4 %collective-permute-done.2.outer_ref = f32[10,24,128]{2,1,0:T(8,128)S(1)} collective-permute-done((f32[10,24,128]{2,1,0:T(8,128)S(1)}, f32[10,24,128]{2,1,0:T(8,128)S(1)}, u32[]{:S(2)}, u32[]{:S(2)}) %collective-permute-start.2) | collective-permute-done | bytes 122912 | tf_op jit(solution)/shard_map/ppermute | solution.py:300
  20.0 0.0 copy-done.1
  20.0 1.1 %shard_map.61 = (f32[19,2,16,128]{3,2,1,0:T(8,128)}, f32[256,128]{1,0:T(8,128)S(1)}) custom-call(s32[1]{0:T(128)} %bitcast.odd_ref, f32[2,19,24,128]{3,2,1,0:T(8,128)S(1)} %get-tuple-element.9.passed_ref, f32[10,24,128]{2,1,0:T(8,128)S(1)} %get-tuple-element.10.up_ref, f32[10,24,128]{2,1,0:T(8,128)S(1)} %get-tuple-element.11.down_ref, ...), custom_call_target="tpu_custom_call" | custom-call | tf_op jit(solution)/shard_map/pallas_call | solution.py:267
  21.1 0.0 copy-start.2
  21.1 17.1 %all_to_all.16 = f32[16,16,128]{2,1,0:T(8,128)S(1)} all-to-all(f32[16,16,128]{2,1,0:T(8,128)S(1)} %bitcast.5), channel_id=1, replica_groups={{0,2,4,6,8,10,12,14,16,18,20,22,24,26,28,30},{32,34,36,38,40,42,44,46,4..., dimensions={0} | all-to-all | bytes 262144 | tf_op jit(solution)/shard_map/all_to_all | solution.py:311
  38.2 0.0 copy-done.2
  38.2 0.6 shard_map.62
  38.8 23.2 %all_to_all.17.got_ref = f32[16,4,128]{2,1,0:T(4,128)S(1)} all-to-all(f32[16,4,128]{2,1,0:T(4,128)S(1)} %shard_map.62), channel_id=1, replica_groups={{0,32,64,96,128,160,192,224,256,288,320,352,384,416,448,480},{2,34,66,9..., dimensions={0} | all-to-all | bytes 65536 | tf_op jit(solution)/shard_map/all_to_all | solution.py:313
  62.1 0.7 %shard_map.63 = f32[4,2,64]{2,1,0:T(2,128)} custom-call(f32[16,4,128]{2,1,0:T(4,128)S(1)} %all_to_all.17.got_ref), custom_call_target="tpu_custom_call" | custom-call | tf_op jit(solution)/shard_map/pallas_call | solution.py:267
Async XLA Ops:
  0.6 4.4 %copy-start = (f32[19,2,16,128]{3,2,1,0:T(8,128)S(1)}, f32[19,2,16,128]{3,2,1,0:T(8,128)}, u32[]{:S(2)}) copy-start(f32[19,2,16,128]{3,2,1,0:T(8,128)} %pops_ref.1) | copy-start | bytes 933892
  1.7 3.3 %copy-start.3 = (s32[2,16,128]{2,1,0:T(8,128)S(1)}, s32[2,16,128]{2,1,0:T(8,128)}, u32[]{:S(2)}) copy-start(s32[2,16,128]{2,1,0:T(8,128)} %flags_ref.1) | copy-start | bytes 49156
  1.7 3.3 %collective-permute-start = (f32[20,2,8,128]{3,2,1,0:T(8,128)S(1)}, f32[20,2,8,128]{3,2,1,0:T(8,128)S(1)}, u32[]{:S(2)}, u32[]{:S(2)}) collective-permute-start(f32[20,2,8,128]{3,2,1,0:T(8,128)S(1)} %shard_map.59), channel_id=1, source_target_pairs={{0,1},{1,0},{2,3},{3,2},{4,5},{5,4},{6,7},{7,6},{8,9},{9,8},{10,11... | collective-permute-start | bytes 491528 | tf_op jit(solution)/shard_map/ppermute | solution.py:293
  3.7 16.4 %copy-start.1 = (f32[256,256]{1,0:T(8,128)S(1)}, f32[256,256]{1,0:T(8,128)}, u32[]{:S(2)}) copy-start(f32[256,256]{1,0:T(8,128)} %constant.23.clone.table_ref) | copy-start | bytes 786436
  5.3 11.4 %collective-permute-start.1 = (f32[10,24,128]{2,1,0:T(8,128)S(1)}, f32[10,24,128]{2,1,0:T(8,128)S(1)}, u32[]{:S(2)}, u32[]{:S(2)}) collective-permute-start(f32[10,24,128]{2,1,0:T(8,128)S(1)} %get-tuple-element.12), channel_id=1, source_target_pairs={{0,2},{2,0},{4,6},{6,4},{8,10},{10,8},{12,14},{14,12},{16,18},{18,... | collective-permute-start | bytes 368648 | tf_op jit(solution)/shard_map/ppermute | solution.py:301
  13.1 7.0 %collective-permute-start.2 = (f32[10,24,128]{2,1,0:T(8,128)S(1)}, f32[10,24,128]{2,1,0:T(8,128)S(1)}, u32[]{:S(2)}, u32[]{:S(2)}) collective-permute-start(f32[10,24,128]{2,1,0:T(8,128)S(1)} %get-tuple-element.13), channel_id=1, source_target_pairs={{0,510},{2,4},{4,2},{6,8},{8,6},{10,12},{12,10},{14,16},{16,14},{1... | collective-permute-start | bytes 368648 | tf_op jit(solution)/shard_map/ppermute | solution.py:300
  21.1 17.1 %copy-start.2 = (f32[128,256]{1,0:T(8,128)S(1)}, f32[128,256]{1,0:T(8,128)}, u32[]{:S(2)}) copy-start(f32[128,256]{1,0:T(8,128)} %constant.24.clone.table_ref) | copy-start | bytes 393220

commit v5 on v3

--- a/solution.py
+++ b/solution.py
@@ -30,6 +30,7 @@
 DOWN_SLOT = {d: k for k, d in enumerate(DOWN)}
 
 VMEM_BYTES = 12 << 20
+RUNS = 8
 HALO = 4
 
 
@@ -81,10 +82,10 @@
 
 
 def edge_kernel(pops_hbm, flags_hbm, edge_ref, pops_ref, flags_ref, sems):
-    copies = [
-        pltpu.make_async_copy(pops_hbm, pops_ref, sems.at[0]),
-        pltpu.make_async_copy(flags_hbm, flags_ref, sems.at[1]),
-    ]
+    copies = [pltpu.make_async_copy(flags_hbm, flags_ref, sems.at[0])]
+    for part in range(4):
+        some = pl.ds(5 * part, min(5, len(DIRS) - 5 * part))
+        copies.append(pltpu.make_async_copy(pops_hbm.at[some], pops_ref.at[some], sems.at[1 + part]))
     for copy in copies:
         copy.start()
     for copy in copies:
@@ -143,8 +144,8 @@
 
 def second_kernel(
     odd_ref, passed_ref, up_ref, down_ref, inner_ref, outer_ref, table_ref,
-    final_ref, send_ref,
-    below_ref, above_ref, relaxed_ref, spread_ref,
+    final_hbm, send_ref,
+    below_ref, above_ref, relaxed_ref, spread_ref, final_ref, sems,
 ):
     odd = jnp.full(up_ref.shape[1:], odd_ref[0]) == 1
     for slot in range(UNITS):
@@ -168,12 +169,15 @@
             out = relax(total, state, near[FLAG, rows] > 0.5, wanted)
             for i in wanted:
                 relaxed_ref[plane, i, rows] = out[i]
+    copies = []
     for plane in range(2):
         total = None
         for i, direction in enumerate(DIRS):
             value = shifted(relaxed_ref[plane + 1 - direction[2], i], direction)
-            final_ref[i, plane] = value[0:16]
+            final_ref[plane, i] = value[0:16]
             total = add_moments(total, {i: value})
+        copies.append(pltpu.make_async_copy(final_ref.at[plane], final_hbm.at[:, plane], sems.at[plane]))
+        copies[-1].start()
         inverse = 1.0 / total[0]
         velocity = [part * inverse for part in total[1:]]
         scalar = SPEED_GAIN * (velocity[0] * velocity[0] + velocity[1] * velocity[1] + velocity[2] * velocity[2])
@@ -186,20 +190,19 @@
         precision=lax.Precision.HIGHEST,
         preferred_element_type=jnp.float32,
     )
+    for copy in copies:
+        copy.wait()
 
 
 def render_kernel(total_planes, got_ref, table_ref, image_ref):
-    slabs = got_ref.shape[0]
-    groups = slabs // 8
-    ordered = jnp.concatenate([got_ref[pl.ds(j, 8, stride=groups), :] for j in range(groups)], axis=0)
     samples = jnp.dot(
-        ordered, table_ref[...], precision=lax.Precision.HIGHEST, preferred_element_type=jnp.float32
-    )
-    depth = jnp.zeros((8, 128), jnp.float32)
-    light = [jnp.zeros((8, 128), jnp.float32) for _ in range(3)]
-    for j in range(groups):
+        got_ref[...], table_ref[...], precision=lax.Precision.HIGHEST, preferred_element_type=jnp.float32
+    )
+    depth = jnp.zeros((RUNS, 128), jnp.float32)
+    light = [jnp.zeros((RUNS, 128), jnp.float32) for _ in range(3)]
+    for step in range(got_ref.shape[0] // RUNS):
         for plane in range(2):
-            sample = samples[8 * j : 8 * j + 8, 128 * plane : 128 * plane + 128]
+            sample = samples[RUNS * step : RUNS * (step + 1), 128 * plane : 128 * plane + 128]
             squared = sample * sample
             green = 1.0 / (1.0 + squared)
             saturation = squared * green
@@ -213,7 +216,7 @@
             light[1] = light[1] + weight * green
             light[2] = light[2] + weight * blue
             depth = depth + extinction
-    row = lax.broadcasted_iota(jnp.int32, (8, 128), 0)
+    row = lax.broadcasted_iota(jnp.int32, (RUNS, 128), 0)
     ahead = depth
     for step in (1, 2, 4):
         ahead = ahead + jnp.where(row >= step, pltpu.roll(ahead, step, 0), 0.0)
@@ -235,12 +238,12 @@
     )
 
 
-def x_table(nodes):
+def x_table(nodes, order):
     table = np.zeros((2 * nodes, 2 * nodes), np.float32)
     for fine in range(4 * nodes):
         for offset, weight in zip((-1, 0, 1, 2), cubic_weights(fine - 2)):
             table[fine // 2, (fine % 2) * nodes + ((fine - 2) // 4 + offset) % nodes] += weight
-    return table
+    return table[order]
 
 
 def y_table(rows):
@@ -255,7 +258,7 @@
     return table
 
 
-def call(kernel, outs, scratch=(), spaces=None):
+def call(kernel, outs, scratch=(), spaces=None, out_spaces=None):
     vmem = pl.BlockSpec(memory_space=pltpu.VMEM)
 
     def run(*operands):
@@ -264,7 +267,7 @@
             kernel,
             out_shape=shapes,
             in_specs=[pl.BlockSpec(memory_space=space) for space in spaces] if spaces else [vmem] * len(operands),
-            out_specs=[vmem] * len(outs),
+            out_specs=[pl.BlockSpec(memory_space=space) for space in out_spaces] if out_spaces else [vmem] * len(outs),
             scratch_shapes=[pltpu.VMEM(part, jnp.float32) if isinstance(part, tuple) else part for part in scratch],
             compiler_params=pltpu.CompilerParams(vmem_limit_bytes=VMEM_BYTES),
         )(*operands)
@@ -276,13 +279,14 @@
     slabs = lax.axis_size("slab")
     dirs, planes, rows, nodes = populations.shape
     held = rows + 2 * HALO
+    order = [(slabs // RUNS) * (row % RUNS) + row // RUNS for row in range(slabs)]
     (edge,) = call(
         edge_kernel,
         [(dirs + 1, planes, 8, nodes)],
         scratch=[
             populations.shape,
             pltpu.VMEM(wall_flags.shape, jnp.int32),
-            pltpu.SemaphoreType.DMA((2,)),
+            pltpu.SemaphoreType.DMA((5,)),
         ],
         spaces=[pltpu.HBM] * 2,
     )(*(pltpu.with_memory_space_constraint(part, pltpu.HBM) for part in (populations, wall_flags)))
@@ -298,10 +302,14 @@
     final, send = call(
         second_kernel,
         [populations.shape, (slabs, 128)],
-        scratch=[message, message, (4, dirs, held, nodes), (128, 256)],
+        scratch=[
+            message, message, (4, dirs, held, nodes), (128, 256), (2, dirs, rows, nodes),
+            pltpu.SemaphoreType.DMA((2,)),
+        ],
         spaces=[pltpu.SMEM] + [pltpu.VMEM] * 6,
-    )(odd, passed, up, down, inner, outer, jnp.asarray(x_table(nodes)))
-    got = lax.all_to_all(send, "slab", 0, 0, tiled=True)
+        out_spaces=[pltpu.HBM, pltpu.VMEM],
+    )(odd, passed, up, down, inner, outer, jnp.asarray(x_table(nodes, order)))
+    got = lax.all_to_all(send, "slab", 0, 0, axis_index_groups=[order], tiled=True)
     (image,) = call(
         functools.partial(render_kernel, planes * slabs), [(4, 2, 4 * rows)]
     )(got, jnp.asarray(y_table(rows)))

time: 62.1 us -> 62 us (level)
  the two profiles are of different devices: /device:TPU:2 before, /device:TPU:8 now
where the time goes in v5:
time: 62 us; the launch traced here: 61.7 us
  blocking collectives  41.8 us (67%)
  starting transfers between devices  9.21 us (15%)
  waiting for transfers between devices  6.52 us (11%)
  Pallas kernels  3.5 us (6%)
  between operations  0.73 us (1%)
    all_to_all x1, blocking collectives, body(): lax.all_to_all(send, 'slab', 0, 0, axis_index_groups=[order], tiled=True)  41.8 us
    ppermute x1, waiting for transfers between devices, body(): lax.ppermute(outer, 'slab', [(i, (i + (1 if i % 2 else -1)) % slabs) for...  5.18 us
    ppermute x1, starting transfers between devices, body(): lax.ppermute(outer, 'slab', [(i, (i + (1 if i % 2 else -1)) % slabs) for...  3.89 us
    pallas_call x4, Pallas kernels, run(): pl.pallas_call(kernel, out_shape=shapes, in_specs=[pl.BlockSpec(memory_sp...  3.5 us
    ppermute x1, starting transfers between devices, body(): inner = lax.ppermute(inner, 'slab', [(i, i ^ 1) for i in range(slabs)])  3.4 us
    ppermute x1, starting transfers between devices, body(): edge = lax.ppermute(edge, 'col', [(0, 1), (1, 0)])  1.92 us
    ppermute x1, waiting for transfers between devices, body(): edge = lax.ppermute(edge, 'col', [(0, 1), (1, 0)])  1.34 us
  transfers between devices with their start and end apart: 3, of which 2 were waited for; matrix products, arithmetic and copies ran while one was open for 0% of the time, Pallas kernels for 0%

profile of v5, /device:TPU:8, one launch (start us, length us, event | category | flops | bytes accessed | tf_op | source)
XLA Modules:
  0.0 61.7 jit_solution(12231218621210303724)
XLA Ops:
  0.6 0.0 copy-start
  0.6 1.1 %shard_map.59 = f32[20,2,8,128]{3,2,1,0:T(8,128)S(1)} custom-call(f32[19,2,16,128]{3,2,1,0:T(8,128)} %pops_ref.1, s32[2,16,128]{2,1,0:T(8,128)} %flags_ref.1), custom_call_target="tpu_custom_call" | custom-call | tf_op jit(solution)/shard_map/pallas_call | solution.py:266
  1.7 0.0 copy-start.3
  1.8 1.9 %collective-permute-start = (f32[20,2,8,128]{3,2,1,0:T(8,128)S(1)}, f32[20,2,8,128]{3,2,1,0:T(8,128)S(1)}, u32[]{:S(2)}, u32[]{:S(2)}) collective-permute-start(f32[20,2,8,128]{3,2,1,0:T(8,128)S(1)} %shard_map.59), channel_id=1, source_target_pairs={{0,1},{1,0},{2,3},{3,2},{4,5},{5,4},{6,7},{7,6},{8,9},{9,8},{10,11... | collective-permute-start | bytes 491528 | tf_op jit(solution)/shard_map/ppermute | solution.py:293
  3.7 0.0 copy-start.1
  3.7 1.3 %collective-permute-done.edge_ref = f32[20,2,8,128]{3,2,1,0:T(8,128)S(1)} collective-permute-done((f32[20,2,8,128]{3,2,1,0:T(8,128)S(1)}, f32[20,2,8,128]{3,2,1,0:T(8,128)S(1)}, u32[]{:S(2)}, u32[]{:S(2)}) %collective-permute-start) | collective-permute-done | bytes 163872 | tf_op jit(solution)/shard_map/ppermute | solution.py:293
  5.0 0.0 copy-done
  5.0 0.0 copy-done.3
  5.0 0.2 shard_map.60
  5.3 3.4 %collective-permute-start.1 = (f32[10,24,128]{2,1,0:T(8,128)S(1)}, f32[10,24,128]{2,1,0:T(8,128)S(1)}, u32[]{:S(2)}, u32[]{:S(2)}) collective-permute-start(f32[10,24,128]{2,1,0:T(8,128)S(1)} %get-tuple-element.12), channel_id=1, source_target_pairs={{0,2},{2,0},{4,6},{6,4},{8,10},{10,8},{12,14},{14,12},{16,18},{18,... | collective-permute-start | bytes 368648 | tf_op jit(solution)/shard_map/ppermute | solution.py:301
  8.7 3.9 %collective-permute-start.2 = (f32[10,24,128]{2,1,0:T(8,128)S(1)}, f32[10,24,128]{2,1,0:T(8,128)S(1)}, u32[]{:S(2)}, u32[]{:S(2)}) collective-permute-start(f32[10,24,128]{2,1,0:T(8,128)S(1)} %get-tuple-element.13), channel_id=1, source_target_pairs={{0,510},{2,4},{4,2},{6,8},{8,6},{10,12},{12,10},{14,16},{16,14},{1... | collective-permute-start | bytes 368648 | tf_op jit(solution)/shard_map/ppermute | solution.py:300
  12.6 0.0 collective-permute-done.1.inner_ref
  12.6 5.2 %collective-permute-done.2.outer_ref = f32[10,24,128]{2,1,0:T(8,128)S(1)} collective-permute-done((f32[10,24,128]{2,1,0:T(8,128)S(1)}, f32[10,24,128]{2,1,0:T(8,128)S(1)}, u32[]{:S(2)}, u32[]{:S(2)}) %collective-permute-start.2) | collective-permute-done | bytes 122912 | tf_op jit(solution)/shard_map/ppermute | solution.py:300
  17.8 0.0 copy-done.1
  17.8 0.9 %shard_map.61 = (f32[19,2,16,128]{3,2,1,0:T(8,128)}, f32[256,128]{1,0:T(8,128)S(1)}) custom-call(s32[1]{0:T(128)} %bitcast.odd_ref, f32[2,19,24,128]{3,2,1,0:T(8,128)S(1)} %get-tuple-element.9.passed_ref, f32[10,24,128]{2,1,0:T(8,128)S(1)} %get-tuple-element.10.up_ref, f32[10,24,128]{2,1,0:T(8,128)S(1)} %get-tuple-element.11.down_ref, ...), custom_call_target="tpu_custom_call" | custom-call | tf_op jit(solution)/shard_map/pallas_call | solution.py:266
  18.7 0.0 copy-start.2
  18.8 41.8 %all_to_all.11 = f32[256,1,128]{2,1,0:T(1,128)S(1)} all-to-all(f32[256,1,128]{2,1,0:T(1,128)S(1)} %bitcast.7), channel_id=1, replica_groups={{0,64,128,192,256,320,384,448,2,66,130,194,258,322,386,450,4,68,132,196..., dimensions={0} | all-to-all | bytes 262144 | tf_op jit(solution)/shard_map/all_to_all | solution.py:312
  60.5 0.0 copy-done.2
  60.5 1.2 %shard_map.62 = f32[4,2,64]{2,1,0:T(2,128)} custom-call(f32[256,128]{1,0:T(8,128)S(1)} %bitcast.6, f32[128,256]{1,0:T(8,128)S(1)} %copy-done.2), custom_call_target="tpu_custom_call" | custom-call | tf_op jit(solution)/shard_map/pallas_call | solution.py:266
Async XLA Ops:
  0.6 4.4 %copy-start = (f32[19,2,16,128]{3,2,1,0:T(8,128)S(1)}, f32[19,2,16,128]{3,2,1,0:T(8,128)}, u32[]{:S(2)}) copy-start(f32[19,2,16,128]{3,2,1,0:T(8,128)} %pops_ref.1) | copy-start | bytes 933892
  1.7 3.3 %copy-start.3 = (s32[2,16,128]{2,1,0:T(8,128)S(1)}, s32[2,16,128]{2,1,0:T(8,128)}, u32[]{:S(2)}) copy-start(s32[2,16,128]{2,1,0:T(8,128)} %flags_ref.1) | copy-start | bytes 49156
  1.8 3.3 %collective-permute-start = (f32[20,2,8,128]{3,2,1,0:T(8,128)S(1)}, f32[20,2,8,128]{3,2,1,0:T(8,128)S(1)}, u32[]{:S(2)}, u32[]{:S(2)}) collective-permute-start(f32[20,2,8,128]{3,2,1,0:T(8,128)S(1)} %shard_map.59), channel_id=1, source_target_pairs={{0,1},{1,0},{2,3},{3,2},{4,5},{5,4},{6,7},{7,6},{8,9},{9,8},{10,11... | collective-permute-start | bytes 491528 | tf_op jit(solution)/shard_map/ppermute | solution.py:293
  3.7 14.1 %copy-start.1 = (f32[256,256]{1,0:T(8,128)S(1)}, f32[256,256]{1,0:T(8,128)}, u32[]{:S(2)}) copy-start(f32[256,256]{1,0:T(8,128)} %constant.23.clone.table_ref) | copy-start | bytes 786436
  5.3 7.3 %collective-permute-start.1 = (f32[10,24,128]{2,1,0:T(8,128)S(1)}, f32[10,24,128]{2,1,0:T(8,128)S(1)}, u32[]{:S(2)}, u32[]{:S(2)}) collective-permute-start(f32[10,24,128]{2,1,0:T(8,128)S(1)} %get-tuple-element.12), channel_id=1, source_target_pairs={{0,2},{2,0},{4,6},{6,4},{8,10},{10,8},{12,14},{14,12},{16,18},{18,... | collective-permute-start | bytes 368648 | tf_op jit(solution)/shard_map/ppermute | solution.py:301
  8.7 9.1 %collective-permute-start.2 = (f32[10,24,128]{2,1,0:T(8,128)S(1)}, f32[10,24,128]{2,1,0:T(8,128)S(1)}, u32[]{:S(2)}, u32[]{:S(2)}) collective-permute-start(f32[10,24,128]{2,1,0:T(8,128)S(1)} %get-tuple-element.13), channel_id=1, source_target_pairs={{0,510},{2,4},{4,2},{6,8},{8,6},{10,12},{12,10},{14,16},{16,14},{1... | collective-permute-start | bytes 368648 | tf_op jit(solution)/shard_map/ppermute | solution.py:300
  18.7 41.8 %copy-start.2 = (f32[128,256]{1,0:T(8,128)S(1)}, f32[128,256]{1,0:T(8,128)}, u32[]{:S(2)}) copy-start(f32[128,256]{1,0:T(8,128)} %constant.24.clone.table_ref) | copy-start | bytes 393220

commit v6 on v5

--- a/solution.py
+++ b/solution.py
@@ -30,7 +30,8 @@
 DOWN_SLOT = {d: k for k, d in enumerate(DOWN)}
 
 VMEM_BYTES = 12 << 20
-RUNS = 8
+GROUP = 16
+PLANE_ORDER = (8, 0, 9, 1, 10, 2, 11, 3, 12, 4, 13, 5, 14, 6, 15, 7)
 HALO = 4
 
 
@@ -194,33 +195,38 @@
         copy.wait()
 
 
-def render_kernel(total_planes, got_ref, table_ref, image_ref):
+def render_kernel(total_planes, order, got_ref, table_ref, image_ref):
+    runs = len(order)
+    steps = got_ref.shape[0] // runs
+    ordered = jnp.concatenate([got_ref[pl.ds(i, runs, stride=steps), :] for i in range(steps)], axis=0)
     samples = jnp.dot(
-        got_ref[...], table_ref[...], precision=lax.Precision.HIGHEST, preferred_element_type=jnp.float32
-    )
-    depth = jnp.zeros((RUNS, 128), jnp.float32)
-    light = [jnp.zeros((RUNS, 128), jnp.float32) for _ in range(3)]
-    for step in range(got_ref.shape[0] // RUNS):
+        ordered, table_ref[...], precision=lax.Precision.HIGHEST, preferred_element_type=jnp.float32
+    )
+    depth = jnp.zeros((runs, 128), jnp.float32)
+    light = [jnp.zeros((runs, 128), jnp.float32) for _ in range(3)]
+    for step in range(steps):
+        sample = samples[runs * step : runs * (step + 1)]
+        squared = sample * sample
+        green = 1.0 / (1.0 + squared)
+        saturation = squared * green
+        extinction = (OPTICAL / total_planes) * saturation
+        opacity = extinction * (1.0 - extinction * (0.5 - extinction * (1.0 / 6.0 - extinction * (1.0 / 24.0))))
+        blue = jnp.exp(-0.5 * (sample - 1.0) * (sample - 1.0))
         for plane in range(2):
-            sample = samples[RUNS * step : RUNS * (step + 1), 128 * plane : 128 * plane + 128]
-            squared = sample * sample
-            green = 1.0 / (1.0 + squared)
-            saturation = squared * green
-            extinction = (OPTICAL / total_planes) * saturation
-            opacity = extinction * (
-                1.0 - extinction * (0.5 - extinction * (1.0 / 6.0 - extinction * (1.0 / 24.0)))
-            )
-            blue = jnp.exp(-0.5 * (sample - 1.0) * (sample - 1.0))
-            weight = jnp.exp(-depth) * opacity
-            light[0] = light[0] + weight * saturation
-            light[1] = light[1] + weight * green
-            light[2] = light[2] + weight * blue
-            depth = depth + extinction
-    row = lax.broadcasted_iota(jnp.int32, (RUNS, 128), 0)
-    ahead = depth
-    for step in (1, 2, 4):
-        ahead = ahead + jnp.where(row >= step, pltpu.roll(ahead, step, 0), 0.0)
-    through = jnp.exp(depth - ahead)
+            lanes = slice(128 * plane, 128 * plane + 128)
+            weight = jnp.exp(-depth) * opacity[:, lanes]
+            light[0] = light[0] + weight * saturation[:, lanes]
+            light[1] = light[1] + weight * green[:, lanes]
+            light[2] = light[2] + weight * blue[:, lanes]
+            depth = depth + extinction[:, lanes]
+    row = lax.broadcasted_iota(jnp.int32, (runs, 128), 0)
+    place = jnp.zeros((runs, 128), jnp.int32)
+    for k, plane in enumerate(order):
+        place = jnp.where(row == k, plane, place)
+    ahead = jnp.zeros((runs, 128), jnp.float32)
+    for k, plane in enumerate(order):
+        ahead = ahead + jnp.where(place > plane, depth[k : k + 1], 0.0)
+    through = jnp.exp(-ahead)
     sums = [jnp.sum(part * through, axis=0, keepdims=True) for part in light]
     sums.append(1.0 - jnp.exp(-jnp.sum(depth, axis=0, keepdims=True)))
     for channel, value in enumerate(sums):
@@ -279,7 +285,7 @@
     slabs = lax.axis_size("slab")
     dirs, planes, rows, nodes = populations.shape
     held = rows + 2 * HALO
-    order = [(slabs // RUNS) * (row % RUNS) + row // RUNS for row in range(slabs)]
+    order = [GROUP * plane + i for plane in PLANE_ORDER for i in range(GROUP)]
     (edge,) = call(
         edge_kernel,
         [(dirs + 1, planes, 8, nodes)],
@@ -311,7 +317,7 @@
     )(odd, passed, up, down, inner, outer, jnp.asarray(x_table(nodes, order)))
     got = lax.all_to_all(send, "slab", 0, 0, axis_index_groups=[order], tiled=True)
     (image,) = call(
-        functools.partial(render_kernel, planes * slabs), [(4, 2, 4 * rows)]
+        functools.partial(render_kernel, planes * slabs, PLANE_ORDER), [(4, 2, 4 * rows)]
     )(got, jnp.asarray(y_table(rows)))
     return jnp.transpose(image, (0, 2, 1)), final
 

time: 62 us -> 57.8 us (0.932)
  the two profiles are of different devices: /device:TPU:8 before, /device:TPU:32 now
where the time goes in v6:
time: 57.8 us; the launch traced here: 57.5 us
  blocking collectives  35.4 us (61%)
  starting transfers between devices  11.3 us (20%)
  waiting for transfers between devices  6.52 us (11%)
  Pallas kernels  3.51 us (6%)
  between operations  0.73 us (1%)
    all_to_all x1, blocking collectives, body(): lax.all_to_all(send, 'slab', 0, 0, axis_index_groups=[order], tiled=True)  35.4 us
    ppermute x1, starting transfers between devices, body(): lax.ppermute(outer, 'slab', [(i, (i + (1 if i % 2 else -1)) % slabs) for...  6 us
    ppermute x1, waiting for transfers between devices, body(): lax.ppermute(outer, 'slab', [(i, (i + (1 if i % 2 else -1)) % slabs) for...  5.18 us
    pallas_call x4, Pallas kernels, run(): pl.pallas_call(kernel, out_shape=shapes, in_specs=[pl.BlockSpec(memory_sp...  3.51 us
    ppermute x1, starting transfers between devices, body(): inner = lax.ppermute(inner, 'slab', [(i, i ^ 1) for i in range(slabs)])  3.4 us
    ppermute x1, starting transfers between devices, body(): edge = lax.ppermute(edge, 'col', [(0, 1), (1, 0)])  1.92 us
    ppermute x1, waiting for transfers between devices, body(): edge = lax.ppermute(edge, 'col', [(0, 1), (1, 0)])  1.34 us
  transfers between devices with their start and end apart: 3, of which 2 were waited for; matrix products, arithmetic and copies ran while one was open for 0% of the time, Pallas kernels for 0%

profile of v6, /device:TPU:32, one launch (start us, length us, event | category | flops | bytes accessed | tf_op | source)
XLA Modules:
  0.0 57.5 jit_solution(1085035365449440217)
XLA Ops:
  0.6 0.0 copy-start
  0.6 1.1 %shard_map.59 = f32[20,2,8,128]{3,2,1,0:T(8,128)S(1)} custom-call(f32[19,2,16,128]{3,2,1,0:T(8,128)} %pops_ref.1, s32[2,16,128]{2,1,0:T(8,128)} %flags_ref.1), custom_call_target="tpu_custom_call" | custom-call | tf_op jit(solution)/shard_map/pallas_call | solution.py:272
  1.7 0.0 copy-start.3
  1.8 1.9 %collective-permute-start = (f32[20,2,8,128]{3,2,1,0:T(8,128)S(1)}, f32[20,2,8,128]{3,2,1,0:T(8,128)S(1)}, u32[]{:S(2)}, u32[]{:S(2)}) collective-permute-start(f32[20,2,8,128]{3,2,1,0:T(8,128)S(1)} %shard_map.59), channel_id=1, source_target_pairs={{0,1},{1,0},{2,3},{3,2},{4,5},{5,4},{6,7},{7,6},{8,9},{9,8},{10,11... | collective-permute-start | bytes 491528 | tf_op jit(solution)/shard_map/ppermute | solution.py:299
  3.7 0.0 copy-start.1
  3.7 1.3 %collective-permute-done.edge_ref = f32[20,2,8,128]{3,2,1,0:T(8,128)S(1)} collective-permute-done((f32[20,2,8,128]{3,2,1,0:T(8,128)S(1)}, f32[20,2,8,128]{3,2,1,0:T(8,128)S(1)}, u32[]{:S(2)}, u32[]{:S(2)}) %collective-permute-start) | collective-permute-done | bytes 163872 | tf_op jit(solution)/shard_map/ppermute | solution.py:299
  5.0 0.0 copy-done
  5.0 0.0 copy-done.3
  5.0 0.2 shard_map.60
  5.3 3.4 %collective-permute-start.1 = (f32[10,24,128]{2,1,0:T(8,128)S(1)}, f32[10,24,128]{2,1,0:T(8,128)S(1)}, u32[]{:S(2)}, u32[]{:S(2)}) collective-permute-start(f32[10,24,128]{2,1,0:T(8,128)S(1)} %get-tuple-element.12), channel_id=1, source_target_pairs={{0,2},{2,0},{4,6},{6,4},{8,10},{10,8},{12,14},{14,12},{16,18},{18,... | collective-permute-start | bytes 368648 | tf_op jit(solution)/shard_map/ppermute | solution.py:307
  8.7 6.0 %collective-permute-start.2 = (f32[10,24,128]{2,1,0:T(8,128)S(1)}, f32[10,24,128]{2,1,0:T(8,128)S(1)}, u32[]{:S(2)}, u32[]{:S(2)}) collective-permute-start(f32[10,24,128]{2,1,0:T(8,128)S(1)} %get-tuple-element.13), channel_id=1, source_target_pairs={{0,510},{2,4},{4,2},{6,8},{8,6},{10,12},{12,10},{14,16},{16,14},{1... | collective-permute-start | bytes 368648 | tf_op jit(solution)/shard_map/ppermute | solution.py:306
  14.7 0.0 collective-permute-done.1.inner_ref
  14.7 5.2 %collective-permute-done.2.outer_ref = f32[10,24,128]{2,1,0:T(8,128)S(1)} collective-permute-done((f32[10,24,128]{2,1,0:T(8,128)S(1)}, f32[10,24,128]{2,1,0:T(8,128)S(1)}, u32[]{:S(2)}, u32[]{:S(2)}) %collective-permute-start.2) | collective-permute-done | bytes 122912 | tf_op jit(solution)/shard_map/ppermute | solution.py:306
  19.9 0.0 copy-done.1
  19.9 0.9 %shard_map.61 = (f32[19,2,16,128]{3,2,1,0:T(8,128)}, f32[256,128]{1,0:T(8,128)S(1)}) custom-call(s32[1]{0:T(128)} %bitcast.odd_ref, f32[2,19,24,128]{3,2,1,0:T(8,128)S(1)} %get-tuple-element.9.passed_ref, f32[10,24,128]{2,1,0:T(8,128)S(1)} %get-tuple-element.10.up_ref, f32[10,24,128]{2,1,0:T(8,128)S(1)} %get-tuple-element.11.down_ref, ...), custom_call_target="tpu_custom_call" | custom-call | tf_op jit(solution)/shard_map/pallas_call | solution.py:272
  20.8 0.0 copy-start.2
  20.9 35.4 %all_to_all.11 = f32[256,1,128]{2,1,0:T(1,128)S(1)} all-to-all(f32[256,1,128]{2,1,0:T(1,128)S(1)} %bitcast.7), channel_id=1, replica_groups={{256,258,260,262,264,266,268,270,272,274,276,278,280,282,284,286,0,2,4,..., dimensions={0} | all-to-all | bytes 262144 | tf_op jit(solution)/shard_map/all_to_all | solution.py:318
  56.3 0.0 copy-done.2
  56.3 1.2 %shard_map.62 = f32[4,2,64]{2,1,0:T(2,128)} custom-call(f32[256,128]{1,0:T(8,128)S(1)} %bitcast.6, f32[128,256]{1,0:T(8,128)S(1)} %copy-done.2), custom_call_target="tpu_custom_call" | custom-call | tf_op jit(solution)/shard_map/pallas_call | solution.py:272
Async XLA Ops:
  0.6 4.4 %copy-start = (f32[19,2,16,128]{3,2,1,0:T(8,128)S(1)}, f32[19,2,16,128]{3,2,1,0:T(8,128)}, u32[]{:S(2)}) copy-start(f32[19,2,16,128]{3,2,1,0:T(8,128)} %pops_ref.1) | copy-start | bytes 933892
  1.7 3.3 %copy-start.3 = (s32[2,16,128]{2,1,0:T(8,128)S(1)}, s32[2,16,128]{2,1,0:T(8,128)}, u32[]{:S(2)}) copy-start(s32[2,16,128]{2,1,0:T(8,128)} %flags_ref.1) | copy-start | bytes 49156
  1.8 3.3 %collective-permute-start = (f32[20,2,8,128]{3,2,1,0:T(8,128)S(1)}, f32[20,2,8,128]{3,2,1,0:T(8,128)S(1)}, u32[]{:S(2)}, u32[]{:S(2)}) collective-permute-start(f32[20,2,8,128]{3,2,1,0:T(8,128)S(1)} %shard_map.59), channel_id=1, source_target_pairs={{0,1},{1,0},{2,3},{3,2},{4,5},{5,4},{6,7},{7,6},{8,9},{9,8},{10,11... | collective-permute-start | bytes 491528 | tf_op jit(solution)/shard_map/ppermute | solution.py:299
  3.7 16.2 %copy-start.1 = (f32[256,256]{1,0:T(8,128)S(1)}, f32[256,256]{1,0:T(8,128)}, u32[]{:S(2)}) copy-start(f32[256,256]{1,0:T(8,128)} %constant.23.clone.table_ref) | copy-start | bytes 786436
  5.3 9.4 %collective-permute-start.1 = (f32[10,24,128]{2,1,0:T(8,128)S(1)}, f32[10,24,128]{2,1,0:T(8,128)S(1)}, u32[]{:S(2)}, u32[]{:S(2)}) collective-permute-start(f32[10,24,128]{2,1,0:T(8,128)S(1)} %get-tuple-element.12), channel_id=1, source_target_pairs={{0,2},{2,0},{4,6},{6,4},{8,10},{10,8},{12,14},{14,12},{16,18},{18,... | collective-permute-start | bytes 368648 | tf_op jit(solution)/shard_map/ppermute | solution.py:307
  8.7 11.2 %collective-permute-start.2 = (f32[10,24,128]{2,1,0:T(8,128)S(1)}, f32[10,24,128]{2,1,0:T(8,128)S(1)}, u32[]{:S(2)}, u32[]{:S(2)}) collective-permute-start(f32[10,24,128]{2,1,0:T(8,128)S(1)} %get-tuple-element.13), channel_id=1, source_target_pairs={{0,510},{2,4},{4,2},{6,8},{8,6},{10,12},{12,10},{14,16},{16,14},{1... | collective-permute-start | bytes 368648 | tf_op jit(solution)/shard_map/ppermute | solution.py:306
  20.8 35.5 %copy-start.2 = (f32[128,256]{1,0:T(8,128)S(1)}, f32[128,256]{1,0:T(8,128)}, u32[]{:S(2)}) copy-start(f32[128,256]{1,0:T(8,128)} %constant.24.clone.table_ref) | copy-start | bytes 393220

commit v7 on v6

--- a/solution.py
+++ b/solution.py
@@ -31,7 +31,8 @@
 
 VMEM_BYTES = 12 << 20
 GROUP = 16
-PLANE_ORDER = (8, 0, 9, 1, 10, 2, 11, 3, 12, 4, 13, 5, 14, 6, 15, 7)
+PLANE_ORDER = (10, 11, 12, 13, 14, 15, 0, 1, 2, 3, 4, 5, 6, 7, 8, 9)
+FIRST = 11
 HALO = 4
 
 
@@ -144,13 +145,13 @@
 
 
 def second_kernel(
-    odd_ref, passed_ref, up_ref, down_ref, inner_ref, outer_ref, table_ref,
+    odd_ref, passed_ref, up_ref, down_ref, early_ref, late_ref, outer_ref, table_ref,
     final_hbm, send_ref,
     below_ref, above_ref, relaxed_ref, spread_ref, final_ref, sems,
 ):
     odd = jnp.full(up_ref.shape[1:], odd_ref[0]) == 1
     for slot in range(UNITS):
-        inner, outer = inner_ref[slot], outer_ref[slot]
+        inner, outer = early_ref[slot] + late_ref[slot], outer_ref[slot]
         below_ref[slot] = jnp.where(odd, inner, outer)
         above_ref[slot] = jnp.where(odd, outer, inner)
     spread_ref[...] = jnp.zeros(spread_ref.shape, jnp.float32)
@@ -198,7 +199,9 @@
 def render_kernel(total_planes, order, got_ref, table_ref, image_ref):
     runs = len(order)
     steps = got_ref.shape[0] // runs
-    ordered = jnp.concatenate([got_ref[pl.ds(i, runs, stride=steps), :] for i in range(steps)], axis=0)
+    ordered = jnp.concatenate(
+        [got_ref[pl.ds((i - FIRST) % steps, runs, stride=steps), :] for i in range(steps)], axis=0
+    )
     samples = jnp.dot(
         ordered, table_ref[...], precision=lax.Precision.HIGHEST, preferred_element_type=jnp.float32
     )
@@ -285,7 +288,7 @@
     slabs = lax.axis_size("slab")
     dirs, planes, rows, nodes = populations.shape
     held = rows + 2 * HALO
-    order = [GROUP * plane + i for plane in PLANE_ORDER for i in range(GROUP)]
+    order = [GROUP * plane + (FIRST + i) % GROUP for plane in PLANE_ORDER for i in range(GROUP)]
     (edge,) = call(
         edge_kernel,
         [(dirs + 1, planes, 8, nodes)],
@@ -303,8 +306,10 @@
     passed, up, down, inner, outer = call(
         first_kernel, [lattice] + [message] * 4, scratch=[lattice], spaces=[pltpu.SMEM] + [pltpu.VMEM] * 3
     )(odd, populations, wall_flags, edge)
+    halves = [[(i, i ^ 1) for i in range(slabs) if i // 2 % 2 == half] for half in range(2)]
+    early = lax.ppermute(inner, "slab", halves[0])
     outer = lax.ppermute(outer, "slab", [(i, (i + (1 if i % 2 else -1)) % slabs) for i in range(slabs)])
-    inner = lax.ppermute(inner, "slab", [(i, i ^ 1) for i in range(slabs)])
+    late = lax.ppermute(inner, "slab", halves[1])
     final, send = call(
         second_kernel,
         [populations.shape, (slabs, 128)],
@@ -312,9 +317,9 @@
             message, message, (4, dirs, held, nodes), (128, 256), (2, dirs, rows, nodes),
             pltpu.SemaphoreType.DMA((2,)),
         ],
-        spaces=[pltpu.SMEM] + [pltpu.VMEM] * 6,
+        spaces=[pltpu.SMEM] + [pltpu.VMEM] * 7,
         out_spaces=[pltpu.HBM, pltpu.VMEM],
-    )(odd, passed, up, down, inner, outer, jnp.asarray(x_table(nodes, order)))
+    )(odd, passed, up, down, early, late, outer, jnp.asarray(x_table(nodes, order)))
     got = lax.all_to_all(send, "slab", 0, 0, axis_index_groups=[order], tiled=True)
     (image,) = call(
         functools.partial(render_kernel, planes * slabs, PLANE_ORDER), [(4, 2, 4 * rows)]

time: 57.8 us -> 56.3 us (0.974)
  the two profiles are of different devices: /device:TPU:32 before, /device:TPU:8 now
where the time goes in v7:
time: 56.3 us; the launch traced here: 56 us
  blocking collectives  36.3 us (64%)
  starting transfers between devices  9.39 us (17%)
  waiting for transfers between devices  6.07 us (11%)
  Pallas kernels  3.52 us (6%)
  between operations  0.73 us (1%)
    all_to_all x1, blocking collectives, body(): lax.all_to_all(send, 'slab', 0, 0, axis_index_groups=[order], tiled=True)  36.3 us
    ppermute x1, starting transfers between devices, body(): lax.ppermute(outer, 'slab', [(i, (i + (1 if i % 2 else -1)) % slabs) for...  4.55 us
    pallas_call x4, Pallas kernels, run(): pl.pallas_call(kernel, out_shape=shapes, in_specs=[pl.BlockSpec(memory_sp...  3.52 us
    ppermute x1, waiting for transfers between devices, body(): early = lax.ppermute(inner, 'slab', halves[0])  2.84 us
    ppermute x1, starting transfers between devices, body(): early = lax.ppermute(inner, 'slab', halves[0])  2.25 us
    ppermute x1, starting transfers between devices, body(): edge = lax.ppermute(edge, 'col', [(0, 1), (1, 0)])  1.92 us
    ppermute x1, waiting for transfers between devices, body(): lax.ppermute(outer, 'slab', [(i, (i + (1 if i % 2 else -1)) % slabs) for...  1.88 us
    ppermute x1, waiting for transfers between devices, body(): edge = lax.ppermute(edge, 'col', [(0, 1), (1, 0)])  1.34 us
  transfers between devices with their start and end apart: 4, of which 3 were waited for; matrix products, arithmetic and copies ran while one was open for 0% of the time, Pallas kernels for 0%

profile of v7, /device:TPU:8, one launch (start us, length us, event | category | flops | bytes accessed | tf_op | source)
XLA Modules:
  0.0 56.0 jit_solution(14915029526901149385)
XLA Ops:
  0.6 0.0 copy-start
  0.6 1.1 %shard_map.59 = f32[20,2,8,128]{3,2,1,0:T(8,128)S(1)} custom-call(f32[19,2,16,128]{3,2,1,0:T(8,128)} %pops_ref.1, s32[2,16,128]{2,1,0:T(8,128)} %flags_ref.1), custom_call_target="tpu_custom_call" | custom-call | tf_op jit(solution)/shard_map/pallas_call | solution.py:275
  1.7 0.0 copy-start.3
  1.8 1.9 %collective-permute-start = (f32[20,2,8,128]{3,2,1,0:T(8,128)S(1)}, f32[20,2,8,128]{3,2,1,0:T(8,128)S(1)}, u32[]{:S(2)}, u32[]{:S(2)}) collective-permute-start(f32[20,2,8,128]{3,2,1,0:T(8,128)S(1)} %shard_map.59), channel_id=1, source_target_pairs={{0,1},{1,0},{2,3},{3,2},{4,5},{5,4},{6,7},{7,6},{8,9},{9,8},{10,11... | collective-permute-start | bytes 491528 | tf_op jit(solution)/shard_map/ppermute | solution.py:302
  3.7 0.0 copy-start.1
  3.7 1.3 %collective-permute-done.edge_ref = f32[20,2,8,128]{3,2,1,0:T(8,128)S(1)} collective-permute-done((f32[20,2,8,128]{3,2,1,0:T(8,128)S(1)}, f32[20,2,8,128]{3,2,1,0:T(8,128)S(1)}, u32[]{:S(2)}, u32[]{:S(2)}) %collective-permute-start) | collective-permute-done | bytes 163872 | tf_op jit(solution)/shard_map/ppermute | solution.py:302
  5.0 0.0 copy-done
  5.0 0.0 copy-done.3
  5.0 0.2 shard_map.60
  5.3 4.6 %collective-permute-start.3 = (f32[10,24,128]{2,1,0:T(8,128)S(1)}, f32[10,24,128]{2,1,0:T(8,128)S(1)}, u32[]{:S(2)}, u32[]{:S(2)}) collective-permute-start(f32[10,24,128]{2,1,0:T(8,128)S(1)} %get-tuple-element.13), channel_id=1, source_target_pairs={{0,510},{2,4},{4,2},{6,8},{8,6},{10,12},{12,10},{14,16},{16,14},{1... | collective-permute-start | bytes 368648 | tf_op jit(solution)/shard_map/ppermute | solution.py:311
  9.8 0.7 %collective-permute-start.2 = (f32[10,24,128]{2,1,0:T(8,128)S(1)}, f32[10,24,128]{2,1,0:T(8,128)S(1)}, u32[]{:S(2)}, u32[]{:S(2)}) collective-permute-start(f32[10,24,128]{2,1,0:T(8,128)S(1)} %get-tuple-element.12), channel_id=1, source_target_pairs={{4,6},{6,4},{12,14},{14,12},{20,22},{22,20},{28,30},{30,28},{36,38... | collective-permute-start | bytes 368648 | tf_op jit(solution)/shard_map/ppermute | solution.py:312
  10.5 2.2 %collective-permute-start.1 = (f32[10,24,128]{2,1,0:T(8,128)S(1)}, f32[10,24,128]{2,1,0:T(8,128)S(1)}, u32[]{:S(2)}, u32[]{:S(2)}) collective-permute-start(f32[10,24,128]{2,1,0:T(8,128)S(1)} %get-tuple-element.12), channel_id=1, source_target_pairs={{0,2},{2,0},{8,10},{10,8},{16,18},{18,16},{24,26},{26,24},{32,34},... | collective-permute-start | bytes 368648 | tf_op jit(solution)/shard_map/ppermute | solution.py:310
  12.8 1.9 %collective-permute-done.3.outer_ref = f32[10,24,128]{2,1,0:T(8,128)S(1)} collective-permute-done((f32[10,24,128]{2,1,0:T(8,128)S(1)}, f32[10,24,128]{2,1,0:T(8,128)S(1)}, u32[]{:S(2)}, u32[]{:S(2)}) %collective-permute-start.3) | collective-permute-done | bytes 122912 | tf_op jit(solution)/shard_map/ppermute | solution.py:311
  14.7 0.0 collective-permute-done.2.late_ref
  14.7 2.8 %collective-permute-done.1.early_ref = f32[10,24,128]{2,1,0:T(8,128)S(1)} collective-permute-done((f32[10,24,128]{2,1,0:T(8,128)S(1)}, f32[10,24,128]{2,1,0:T(8,128)S(1)}, u32[]{:S(2)}, u32[]{:S(2)}) %collective-permute-start.1) | collective-permute-done | bytes 122912 | tf_op jit(solution)/shard_map/ppermute | solution.py:310
  17.5 0.0 copy-done.1
  17.5 1.0 %shard_map.61 = (f32[19,2,16,128]{3,2,1,0:T(8,128)}, f32[256,128]{1,0:T(8,128)S(1)}) custom-call(s32[1]{0:T(128)} %bitcast.odd_ref, f32[2,19,24,128]{3,2,1,0:T(8,128)S(1)} %get-tuple-element.9.passed_ref, f32[10,24,128]{2,1,0:T(8,128)S(1)} %get-tuple-element.10.up_ref, f32[10,24,128]{2,1,0:T(8,128)S(1)} %get-tuple-element.11.down_ref, ...), custom_call_target="tpu_custom_call" | custom-call | tf_op jit(solution)/shard_map/pallas_call | solution.py:275
  18.5 0.0 copy-start.2
  18.5 36.3 %all_to_all.11 = f32[256,1,128]{2,1,0:T(1,128)S(1)} all-to-all(f32[256,1,128]{2,1,0:T(1,128)S(1)} %bitcast.7), channel_id=1, replica_groups={{342,344,346,348,350,320,322,324,326,328,330,332,334,336,338,340,374,37..., dimensions={0} | all-to-all | bytes 262144 | tf_op jit(solution)/shard_map/all_to_all | solution.py:323
  54.8 0.0 copy-done.2
  54.8 1.2 %shard_map.62 = f32[4,2,64]{2,1,0:T(2,128)} custom-call(f32[256,128]{1,0:T(8,128)S(1)} %bitcast.6, f32[128,256]{1,0:T(8,128)S(1)} %copy-done.2), custom_call_target="tpu_custom_call" | custom-call | tf_op jit(solution)/shard_map/pallas_call | solution.py:275
Async XLA Ops:
  0.6 4.4 %copy-start = (f32[19,2,16,128]{3,2,1,0:T(8,128)S(1)}, f32[19,2,16,128]{3,2,1,0:T(8,128)}, u32[]{:S(2)}) copy-start(f32[19,2,16,128]{3,2,1,0:T(8,128)} %pops_ref.1) | copy-start | bytes 933892
  1.7 3.3 %copy-start.3 = (s32[2,16,128]{2,1,0:T(8,128)S(1)}, s32[2,16,128]{2,1,0:T(8,128)}, u32[]{:S(2)}) copy-start(s32[2,16,128]{2,1,0:T(8,128)} %flags_ref.1) | copy-start | bytes 49156
  1.8 3.3 %collective-permute-start = (f32[20,2,8,128]{3,2,1,0:T(8,128)S(1)}, f32[20,2,8,128]{3,2,1,0:T(8,128)S(1)}, u32[]{:S(2)}, u32[]{:S(2)}) collective-permute-start(f32[20,2,8,128]{3,2,1,0:T(8,128)S(1)} %shard_map.59), channel_id=1, source_target_pairs={{0,1},{1,0},{2,3},{3,2},{4,5},{5,4},{6,7},{7,6},{8,9},{9,8},{10,11... | collective-permute-start | bytes 491528 | tf_op jit(solution)/shard_map/ppermute | solution.py:302
  3.7 13.8 %copy-start.1 = (f32[256,256]{1,0:T(8,128)S(1)}, f32[256,256]{1,0:T(8,128)}, u32[]{:S(2)}) copy-start(f32[256,256]{1,0:T(8,128)} %constant.23.clone.table_ref) | copy-start | bytes 786436
  5.3 9.4 %collective-permute-start.3 = (f32[10,24,128]{2,1,0:T(8,128)S(1)}, f32[10,24,128]{2,1,0:T(8,128)S(1)}, u32[]{:S(2)}, u32[]{:S(2)}) collective-permute-start(f32[10,24,128]{2,1,0:T(8,128)S(1)} %get-tuple-element.13), channel_id=1, source_target_pairs={{0,510},{2,4},{4,2},{6,8},{8,6},{10,12},{12,10},{14,16},{16,14},{1... | collective-permute-start | bytes 368648 | tf_op jit(solution)/shard_map/ppermute | solution.py:311
  9.8 4.8 %collective-permute-start.2 = (f32[10,24,128]{2,1,0:T(8,128)S(1)}, f32[10,24,128]{2,1,0:T(8,128)S(1)}, u32[]{:S(2)}, u32[]{:S(2)}) collective-permute-start(f32[10,24,128]{2,1,0:T(8,128)S(1)} %get-tuple-element.12), channel_id=1, source_target_pairs={{4,6},{6,4},{12,14},{14,12},{20,22},{22,20},{28,30},{30,28},{36,38... | collective-permute-start | bytes 368648 | tf_op jit(solution)/shard_map/ppermute | solution.py:312
  10.5 7.0 %collective-permute-start.1 = (f32[10,24,128]{2,1,0:T(8,128)S(1)}, f32[10,24,128]{2,1,0:T(8,128)S(1)}, u32[]{:S(2)}, u32[]{:S(2)}) collective-permute-start(f32[10,24,128]{2,1,0:T(8,128)S(1)} %get-tuple-element.12), channel_id=1, source_target_pairs={{0,2},{2,0},{8,10},{10,8},{16,18},{18,16},{24,26},{26,24},{32,34},... | collective-permute-start | bytes 368648 | tf_op jit(solution)/shard_map/ppermute | solution.py:310
  18.5 36.3 %copy-start.2 = (f32[128,256]{1,0:T(8,128)S(1)}, f32[128,256]{1,0:T(8,128)}, u32[]{:S(2)}) copy-start(f32[128,256]{1,0:T(8,128)} %constant.24.clone.table_ref) | copy-start | bytes 393220

commit v8 on v7

--- a/solution.py
+++ b/solution.py
@@ -146,8 +146,8 @@
 
 def second_kernel(
     odd_ref, passed_ref, up_ref, down_ref, early_ref, late_ref, outer_ref, table_ref,
-    final_hbm, send_ref,
-    below_ref, above_ref, relaxed_ref, spread_ref, final_ref, sems,
+    final_ref, send_ref,
+    below_ref, above_ref, relaxed_ref, spread_ref,
 ):
     odd = jnp.full(up_ref.shape[1:], odd_ref[0]) == 1
     for slot in range(UNITS):
@@ -171,15 +171,12 @@
             out = relax(total, state, near[FLAG, rows] > 0.5, wanted)
             for i in wanted:
                 relaxed_ref[plane, i, rows] = out[i]
-    copies = []
     for plane in range(2):
         total = None
         for i, direction in enumerate(DIRS):
             value = shifted(relaxed_ref[plane + 1 - direction[2], i], direction)
             final_ref[plane, i] = value[0:16]
             total = add_moments(total, {i: value})
-        copies.append(pltpu.make_async_copy(final_ref.at[plane], final_hbm.at[:, plane], sems.at[plane]))
-        copies[-1].start()
         inverse = 1.0 / total[0]
         velocity = [part * inverse for part in total[1:]]
         scalar = SPEED_GAIN * (velocity[0] * velocity[0] + velocity[1] * velocity[1] + velocity[2] * velocity[2])
@@ -192,11 +189,12 @@
         precision=lax.Precision.HIGHEST,
         preferred_element_type=jnp.float32,
     )
+
+
+def render_kernel(total_planes, order, got_ref, table_ref, final_ref, image_ref, final_hbm, sems):
+    copies = [pltpu.make_async_copy(final_ref.at[plane], final_hbm.at[:, plane], sems.at[plane]) for plane in range(2)]
     for copy in copies:
-        copy.wait()
-
-
-def render_kernel(total_planes, order, got_ref, table_ref, image_ref):
+        copy.start()
     runs = len(order)
     steps = got_ref.shape[0] // runs
     ordered = jnp.concatenate(
@@ -235,6 +233,8 @@
     for channel, value in enumerate(sums):
         image_ref[channel, 0:1, :] = value[:, 0:64]
         image_ref[channel, 1:2, :] = value[:, 64:128]
+    for copy in copies:
+        copy.wait()
 
 
 def cubic_weights(row):
@@ -312,18 +312,19 @@
     late = lax.ppermute(inner, "slab", halves[1])
     final, send = call(
         second_kernel,
-        [populations.shape, (slabs, 128)],
+        [(planes, dirs, rows, nodes), (slabs, 128)],
         scratch=[
-            message, message, (4, dirs, held, nodes), (128, 256), (2, dirs, rows, nodes),
-            pltpu.SemaphoreType.DMA((2,)),
+            message, message, (4, dirs, held, nodes), (128, 256),
         ],
         spaces=[pltpu.SMEM] + [pltpu.VMEM] * 7,
-        out_spaces=[pltpu.HBM, pltpu.VMEM],
     )(odd, passed, up, down, early, late, outer, jnp.asarray(x_table(nodes, order)))
     got = lax.all_to_all(send, "slab", 0, 0, axis_index_groups=[order], tiled=True)
-    (image,) = call(
-        functools.partial(render_kernel, planes * slabs, PLANE_ORDER), [(4, 2, 4 * rows)]
-    )(got, jnp.asarray(y_table(rows)))
+    image, final = call(
+        functools.partial(render_kernel, planes * slabs, PLANE_ORDER),
+        [(4, 2, 4 * rows), populations.shape],
+        scratch=[pltpu.SemaphoreType.DMA((2,))],
+        out_spaces=[pltpu.VMEM, pltpu.HBM],
+    )(got, jnp.asarray(y_table(rows)), final)
     return jnp.transpose(image, (0, 2, 1)), final
 
 

time: 56.3 us -> 56.1 us (level)
  no operation moved by 1% of the time
where the time goes in v8:
time: 56.1 us; the launch traced here: 55.8 us
  blocking collectives  36.3 us (65%)
  starting transfers between devices  9.39 us (17%)
  waiting for transfers between devices  6.07 us (11%)
  Pallas kernels  3.28 us (6%)
  between operations  0.73 us (1%)
    all_to_all x1, blocking collectives, body(): lax.all_to_all(send, 'slab', 0, 0, axis_index_groups=[order], tiled=True)  36.3 us
    ppermute x1, starting transfers between devices, body(): lax.ppermute(outer, 'slab', [(i, (i + (1 if i % 2 else -1)) % slabs) for...  4.55 us
    pallas_call x4, Pallas kernels, run(): pl.pallas_call(kernel, out_shape=shapes, in_specs=[pl.BlockSpec(memory_sp...  3.28 us
    ppermute x1, waiting for transfers between devices, body(): early = lax.ppermute(inner, 'slab', halves[0])  2.84 us
    ppermute x1, starting transfers between devices, body(): early = lax.ppermute(inner, 'slab', halves[0])  2.25 us
    ppermute x1, starting transfers between devices, body(): edge = lax.ppermute(edge, 'col', [(0, 1), (1, 0)])  1.92 us
    ppermute x1, waiting for transfers between devices, body(): lax.ppermute(outer, 'slab', [(i, (i + (1 if i % 2 else -1)) % slabs) for...  1.88 us
    ppermute x1, waiting for transfers between devices, body(): edge = lax.ppermute(edge, 'col', [(0, 1), (1, 0)])  1.34 us
  transfers between devices with their start and end apart: 4, of which 3 were waited for; matrix products, arithmetic and copies ran while one was open for 0% of the time, Pallas kernels for 0%

profile of v8, /device:TPU:8, one launch (start us, length us, event | category | flops | bytes accessed | tf_op | source)
XLA Modules:
  0.0 55.8 jit_solution(293150169993297952)
XLA Ops:
  0.6 0.0 copy-start
  0.6 1.1 %shard_map.59 = f32[20,2,8,128]{3,2,1,0:T(8,128)S(1)} custom-call(f32[19,2,16,128]{3,2,1,0:T(8,128)} %pops_ref.1, s32[2,16,128]{2,1,0:T(8,128)} %flags_ref.1), custom_call_target="tpu_custom_call" | custom-call | tf_op jit(solution)/shard_map/pallas_call | solution.py:275
  1.7 0.0 copy-start.3
  1.8 1.9 %collective-permute-start = (f32[20,2,8,128]{3,2,1,0:T(8,128)S(1)}, f32[20,2,8,128]{3,2,1,0:T(8,128)S(1)}, u32[]{:S(2)}, u32[]{:S(2)}) collective-permute-start(f32[20,2,8,128]{3,2,1,0:T(8,128)S(1)} %shard_map.59), channel_id=1, source_target_pairs={{0,1},{1,0},{2,3},{3,2},{4,5},{5,4},{6,7},{7,6},{8,9},{9,8},{10,11... | collective-permute-start | bytes 491528 | tf_op jit(solution)/shard_map/ppermute | solution.py:302
  3.7 0.0 copy-start.1
  3.7 1.3 %collective-permute-done.edge_ref = f32[20,2,8,128]{3,2,1,0:T(8,128)S(1)} collective-permute-done((f32[20,2,8,128]{3,2,1,0:T(8,128)S(1)}, f32[20,2,8,128]{3,2,1,0:T(8,128)S(1)}, u32[]{:S(2)}, u32[]{:S(2)}) %collective-permute-start) | collective-permute-done | bytes 163872 | tf_op jit(solution)/shard_map/ppermute | solution.py:302
  5.0 0.0 copy-done
  5.0 0.0 copy-done.3
  5.0 0.2 shard_map.60
  5.3 4.6 %collective-permute-start.3 = (f32[10,24,128]{2,1,0:T(8,128)S(1)}, f32[10,24,128]{2,1,0:T(8,128)S(1)}, u32[]{:S(2)}, u32[]{:S(2)}) collective-permute-start(f32[10,24,128]{2,1,0:T(8,128)S(1)} %get-tuple-element.15), channel_id=1, source_target_pairs={{0,510},{2,4},{4,2},{6,8},{8,6},{10,12},{12,10},{14,16},{16,14},{1... | collective-permute-start | bytes 368648 | tf_op jit(solution)/shard_map/ppermute | solution.py:311
  9.8 0.7 %collective-permute-start.2 = (f32[10,24,128]{2,1,0:T(8,128)S(1)}, f32[10,24,128]{2,1,0:T(8,128)S(1)}, u32[]{:S(2)}, u32[]{:S(2)}) collective-permute-start(f32[10,24,128]{2,1,0:T(8,128)S(1)} %get-tuple-element.14), channel_id=1, source_target_pairs={{4,6},{6,4},{12,14},{14,12},{20,22},{22,20},{28,30},{30,28},{36,38... | collective-permute-start | bytes 368648 | tf_op jit(solution)/shard_map/ppermute | solution.py:312
  10.5 2.2 %collective-permute-start.1 = (f32[10,24,128]{2,1,0:T(8,128)S(1)}, f32[10,24,128]{2,1,0:T(8,128)S(1)}, u32[]{:S(2)}, u32[]{:S(2)}) collective-permute-start(f32[10,24,128]{2,1,0:T(8,128)S(1)} %get-tuple-element.14), channel_id=1, source_target_pairs={{0,2},{2,0},{8,10},{10,8},{16,18},{18,16},{24,26},{26,24},{32,34},... | collective-permute-start | bytes 368648 | tf_op jit(solution)/shard_map/ppermute | solution.py:310
  12.8 1.9 %collective-permute-done.3.outer_ref = f32[10,24,128]{2,1,0:T(8,128)S(1)} collective-permute-done((f32[10,24,128]{2,1,0:T(8,128)S(1)}, f32[10,24,128]{2,1,0:T(8,128)S(1)}, u32[]{:S(2)}, u32[]{:S(2)}) %collective-permute-start.3) | collective-permute-done | bytes 122912 | tf_op jit(solution)/shard_map/ppermute | solution.py:311
  14.7 0.0 collective-permute-done.2.late_ref
  14.7 2.8 %collective-permute-done.1.early_ref = f32[10,24,128]{2,1,0:T(8,128)S(1)} collective-permute-done((f32[10,24,128]{2,1,0:T(8,128)S(1)}, f32[10,24,128]{2,1,0:T(8,128)S(1)}, u32[]{:S(2)}, u32[]{:S(2)}) %collective-permute-start.1) | collective-permute-done | bytes 122912 | tf_op jit(solution)/shard_map/ppermute | solution.py:310
  17.5 0.0 copy-done.1
  17.5 0.6 %shard_map.61 = (f32[2,19,16,128]{3,2,1,0:T(8,128)S(1)}, f32[256,128]{1,0:T(8,128)S(1)}) custom-call(s32[1]{0:T(128)} %bitcast.odd_ref, f32[2,19,24,128]{3,2,1,0:T(8,128)S(1)} %get-tuple-element.11.passed_ref, f32[10,24,128]{2,1,0:T(8,128)S(1)} %get-tuple-element.12.up_ref, f32[10,24,128]{2,1,0:T(8,128)S(1)} %get-tuple-element.13.down_ref, ...), custom_call_target="tpu_custom_call" | custom-call | tf_op jit(solution)/shard_map/pallas_call | solution.py:275
  18.1 0.0 copy-start.2
  18.1 36.3 %all_to_all.11 = f32[256,1,128]{2,1,0:T(1,128)S(1)} all-to-all(f32[256,1,128]{2,1,0:T(1,128)S(1)} %bitcast.7), channel_id=1, replica_groups={{342,344,346,348,350,320,322,324,326,328,330,332,334,336,338,340,374,37..., dimensions={0} | all-to-all | bytes 262144 | tf_op jit(solution)/shard_map/all_to_all | solution.py:321
  54.4 0.0 copy-done.2
  54.4 1.3 %shard_map.62 = (f32[4,2,64]{2,1,0:T(2,128)}, f32[19,2,16,128]{3,2,1,0:T(8,128)}) custom-call(f32[256,128]{1,0:T(8,128)S(1)} %bitcast.6, f32[128,256]{1,0:T(8,128)S(1)} %copy-done.2, f32[2,19,16,128]{3,2,1,0:T(8,128)S(1)} %get-tuple-element.17.final_ref), custom_call_target="tpu_custom_call" | custom-call | tf_op jit(solution)/shard_map/pallas_call | solution.py:275
Async XLA Ops:
  0.6 4.4 %copy-start = (f32[19,2,16,128]{3,2,1,0:T(8,128)S(1)}, f32[19,2,16,128]{3,2,1,0:T(8,128)}, u32[]{:S(2)}) copy-start(f32[19,2,16,128]{3,2,1,0:T(8,128)} %pops_ref.1) | copy-start | bytes 933892
  1.7 3.3 %copy-start.3 = (s32[2,16,128]{2,1,0:T(8,128)S(1)}, s32[2,16,128]{2,1,0:T(8,128)}, u32[]{:S(2)}) copy-start(s32[2,16,128]{2,1,0:T(8,128)} %flags_ref.1) | copy-start | bytes 49156
  1.8 3.3 %collective-permute-start = (f32[20,2,8,128]{3,2,1,0:T(8,128)S(1)}, f32[20,2,8,128]{3,2,1,0:T(8,128)S(1)}, u32[]{:S(2)}, u32[]{:S(2)}) collective-permute-start(f32[20,2,8,128]{3,2,1,0:T(8,128)S(1)} %shard_map.59), channel_id=1, source_target_pairs={{0,1},{1,0},{2,3},{3,2},{4,5},{5,4},{6,7},{7,6},{8,9},{9,8},{10,11... | collective-permute-start | bytes 491528 | tf_op jit(solution)/shard_map/ppermute | solution.py:302
  3.7 13.8 %copy-start.1 = (f32[256,256]{1,0:T(8,128)S(1)}, f32[256,256]{1,0:T(8,128)}, u32[]{:S(2)}) copy-start(f32[256,256]{1,0:T(8,128)} %constant.23.clone.table_ref) | copy-start | bytes 786436
  5.3 9.4 %collective-permute-start.3 = (f32[10,24,128]{2,1,0:T(8,128)S(1)}, f32[10,24,128]{2,1,0:T(8,128)S(1)}, u32[]{:S(2)}, u32[]{:S(2)}) collective-permute-start(f32[10,24,128]{2,1,0:T(8,128)S(1)} %get-tuple-element.15), channel_id=1, source_target_pairs={{0,510},{2,4},{4,2},{6,8},{8,6},{10,12},{12,10},{14,16},{16,14},{1... | collective-permute-start | bytes 368648 | tf_op jit(solution)/shard_map/ppermute | solution.py:311
  9.8 4.8 %collective-permute-start.2 = (f32[10,24,128]{2,1,0:T(8,128)S(1)}, f32[10,24,128]{2,1,0:T(8,128)S(1)}, u32[]{:S(2)}, u32[]{:S(2)}) collective-permute-start(f32[10,24,128]{2,1,0:T(8,128)S(1)} %get-tuple-element.14), channel_id=1, source_target_pairs={{4,6},{6,4},{12,14},{14,12},{20,22},{22,20},{28,30},{30,28},{36,38... | collective-permute-start | bytes 368648 | tf_op jit(solution)/shard_map/ppermute | solution.py:312
  10.5 7.0 %collective-permute-start.1 = (f32[10,24,128]{2,1,0:T(8,128)S(1)}, f32[10,24,128]{2,1,0:T(8,128)S(1)}, u32[]{:S(2)}, u32[]{:S(2)}) collective-permute-start(f32[10,24,128]{2,1,0:T(8,128)S(1)} %get-tuple-element.14), channel_id=1, source_target_pairs={{0,2},{2,0},{8,10},{10,8},{16,18},{18,16},{24,26},{26,24},{32,34},... | collective-permute-start | bytes 368648 | tf_op jit(solution)/shard_map/ppermute | solution.py:310
  18.1 36.3 %copy-start.2 = (f32[128,256]{1,0:T(8,128)S(1)}, f32[128,256]{1,0:T(8,128)}, u32[]{:S(2)}) copy-start(f32[128,256]{1,0:T(8,128)} %constant.24.clone.table_ref) | copy-start | bytes 393220
